TPU v7x, 32 devices: a whole 2x2x4 slice. The times are simulated.
32 devices in a mesh: lvl: 4 (over z), sp: 8 (over y, x, core).
Axes of the slice: x: 2, y: 2, z: 4, core: 2. Of those that a mesh axis runs over, the one named last changes fastest.
Arguments:
- input_field: bfloat16 [3, 800, 128, 128], P(None, 'lvl', 'sp'), may hold values from -6 to 6
- cotangent: bfloat16 [3, 800, 128, 128], P(None, 'lvl', 'sp'), may hold values from -6 to 6
- ocean_mask: int32 [3, 128, 128], P(None, 'sp'), may hold values 0 or 1
- crop_rows: int32 [3, 8], P(None, 'sp'), may hold values from 8 to 16, as said below
- step_count: int32 [], replicated, may hold values from 1 to 20
- kernel: float32 [800, 49], P('lvl'), may hold values from -0.875 to 0.875
- kernel_first: float32 [800, 49], P('lvl'), may hold values from -56 to 56
- kernel_second: float32 [800, 49], P('lvl'), may hold values from 7.86432 to 31.45728
- scales: float32 [2, 800], P(None, 'lvl'), may hold values from 0.5 to 1.5
- scales_first: float32 [2, 800], P(None, 'lvl'), may hold values from -56 to 56
- scales_second: float32 [2, 800], P(None, 'lvl'), may hold values from 7.86432 to 31.45728
- expand: float32 [800, 3200], P(None, 'sp'), may hold values from -0.21875 to 0.21875
- expand_first: float32 [800, 3200], P(None, 'sp'), may hold values from -28 to 28
- expand_second: float32 [800, 3200], P(None, 'sp'), may hold values from 1.96608 to 7.86432
- uplift: float32 [3200], P('sp'), may hold values from -1.75 to 1.75
- uplift_first: float32 [3200], P('sp'), may hold values from -28 to 28
- uplift_second: float32 [3200], P('sp'), may hold values from 1.96608 to 7.86432
- shrink: float32 [3200, 800], P('sp'), may hold values from -0.109375 to 0.109375
- shrink_first: float32 [3200, 800], P('sp'), may hold values from -64 to 64
- shrink_second: float32 [3200, 800], P('sp'), may hold values from 9.8304 to 39.3216
- offset: float32 [800], P('sp'), may hold values from -1.75 to 1.75
- offset_first: float32 [800], P('sp'), may hold values from -112 to 112
- offset_second: float32 [800], P('sp'), may hold values from 27.52512 to 108.1344
Outputs:
- block_output: float32 [3, 800, 128, 128], P(None, 'lvl', 'sp')
- input_grad: float32 [3, 800, 128, 128], P(None, 'lvl', 'sp')
- kernel_grad: float32 [800, 49], P('lvl')
- kernel_moment: float32 [800, 49], P('lvl')
- kernel_next: float32 [800, 49], P('lvl')
- scales_grad: float32 [2, 800], P(None, 'lvl')
- scales_moment: float32 [2, 800], P(None, 'lvl')
- scales_next: float32 [2, 800], P(None, 'lvl')
- expand_grad: float32 [800, 3200], P(None, 'sp')
- expand_moment: float32 [800, 3200], P(None, 'sp')
- expand_next: float32 [800, 3200], P(None, 'sp')
- uplift_grad: float32 [3200], P('sp')
- uplift_moment: float32 [3200], P('sp')
- uplift_next: float32 [3200], P('sp')
- shrink_grad: float32 [3200, 800], P('sp')
- shrink_moment: float32 [3200, 800], P('sp')
- shrink_next: float32 [3200, 800], P('sp')
- offset_grad: float32 [800], P('sp')
- offset_moment: float32 [800], P('sp')
- offset_next: float32 [800], P('sp')
- step_next: int32 [], replicated
Inputs may be any that keep to these rules, and one draw needn't show every extreme that they name: `crop_rows`: at least half of a tile's rows; in each micro-batch some tile keeps all 16.
All inputs are finite; a program needn't handle non-finite values. No bound on the sum of `ocean_mask` on one device may be relied on, other than what follows from the above.
Results may differ from a plain program's by a relative error of at most 0.007.
Values may be sent and summed in bfloat16 or wider, within the bound.
A program may use at most 256 MiB of HBM per device.

v0:
```python
import jax
import jax.numpy as jnp
from jax import lax
from jax.sharding import PartitionSpec as P

KW = 7


beta_one = 0.9
beta_two = 0.999
epsilon = 1e-08
weight_decay = 0.01


def extended(cells, sides, width):
    for axis, dim in sides:
        count = lax.axis_size(axis)
        ends = count - 1
        head = lax.slice_in_dim(cells, 0, width, axis=dim)
        tail = lax.slice_in_dim(cells, cells.shape[dim] - width, cells.shape[dim], axis=dim)
        cells = jnp.concatenate(
            [
                lax.ppermute(tail, axis, [(i, (i + 1) % count) for i in range(ends)]),
                cells,
                lax.ppermute(head, axis, [((i + 1) % count, i) for i in range(ends)]),
            ],
            axis=dim,
        )
    return cells


def adamw(weight, first, second, grad, rate, step_float):
    first_new = beta_one * first + (1.0 - beta_one) * grad
    second_new = beta_two * second + (1.0 - beta_two) * grad * grad
    fix_first = 1.0 - jnp.power(beta_one, step_float)
    fix_second = 1.0 - jnp.power(beta_two, step_float)
    update = (
        first_new / fix_first / (jnp.sqrt(second_new / fix_second) + epsilon)
        + weight_decay * weight
    )
    return (second_new, weight - rate * update)


def depthwise_framed(framed, kernel, height, breadth):
    running = jnp.zeros((framed.shape[0], height, breadth), jnp.float32)
    for vertical in range(KW):
        for lateral in range(KW):
            weights_now = kernel[:, vertical * KW + lateral][:, None, None]
            running = (
                running
                + weights_now * framed[:, vertical : vertical + height, lateral : lateral + breadth]
            )
    return running


def depthwise_back(rimmed, kernel, height, breadth):
    margin = KW // 2
    running = jnp.zeros((rimmed.shape[0], height, breadth), jnp.float32)
    for vertical in range(KW):
        for lateral in range(KW):
            first_row = 2 * margin - vertical
            first_col = 2 * margin - lateral
            weights_now = kernel[:, vertical * KW + lateral][:, None, None]
            running = (
                running
                + weights_now
                * rimmed[:, first_row : first_row + height, first_col : first_col + breadth]
            )
    return running


def kernel_terms(grad_conv, framed, height, breadth):
    columns = []
    for vertical in range(KW):
        for lateral in range(KW):
            columns.append(
                jnp.sum(
                    grad_conv
                    * framed[:, vertical : vertical + height, lateral : lateral + breadth],
                    axis=(1, 2),
                )
            )
    return jnp.stack(columns, axis=1)


def on_device(
    input_field,
    cotangent,
    ocean_mask,
    crop_rows,
    step_count,
    kernel,
    kernel_first,
    kernel_second,
    scales,
    scales_first,
    scales_second,
    expand,
    expand_first,
    expand_second,
    uplift,
    uplift_first,
    uplift_second,
    shrink,
    shrink_first,
    shrink_second,
    offset,
    offset_first,
    offset_second,
):
    batches = input_field.shape[0]
    channels = input_field.shape[1]
    height = input_field.shape[2]
    breadth = input_field.shape[3]
    margin = KW // 2
    expand_all, uplift_all, shrink_all, offset_all = (
        lax.all_gather(expand.astype(jnp.bfloat16), "sp", axis=1, tiled=True),
        lax.all_gather(uplift.astype(jnp.bfloat16), "sp", axis=0, tiled=True),
        lax.all_gather(shrink.astype(jnp.bfloat16), "sp", axis=0, tiled=True),
        lax.all_gather(offset.astype(jnp.bfloat16), "sp", axis=0, tiled=True),
    )
    uplift_wide = uplift_all.astype(jnp.float32)[:, None]
    offset_wide = offset_all.astype(jnp.float32)[:, None]
    gain_rows = scales[0][:, None, None]
    shift_rows = scales[1][:, None, None]
    row_local = jnp.arange(height, dtype=jnp.int32)
    full_expand = jnp.zeros(expand_all.shape, jnp.float32)
    full_uplift = jnp.zeros(uplift_all.shape, jnp.float32)
    full_shrink = jnp.zeros(shrink_all.shape, jnp.float32)
    full_offset = jnp.zeros(offset_all.shape, jnp.float32)
    kernel_local = jnp.zeros(kernel.shape, jnp.float32)
    gain_grad = jnp.zeros((channels,), jnp.float32)
    shift_grad = jnp.zeros((channels,), jnp.float32)
    outputs = []
    input_grads = []
    for batch_index in range(batches):
        valid_rows = (row_local < crop_rows[batch_index, 0]).astype(jnp.float32)[None, :, None]
        field_now = (input_field[batch_index].astype(jnp.float32) * valid_rows).astype(jnp.bfloat16)
        ocean_cells = ocean_mask[batch_index].astype(jnp.float32)[None] * valid_rows
        framed = extended(field_now, (("sp", 1),), margin)
        framed = jnp.pad(framed.astype(jnp.float32), ((0, 0), (0, 0), (margin, margin)))
        convolved = depthwise_framed(framed, kernel, height, breadth)
        local_count = jnp.sum(ocean_cells)
        ocean_sums, count_sum = lax.psum(
            (jnp.sum(ocean_cells * convolved, axis=(1, 2)), local_count), "sp"
        )
        ocean_count = jnp.maximum(count_sum, 1.0)
        mean_value = ocean_sums / ocean_count
        centred = convolved - mean_value[:, None, None]
        spread = lax.psum(jnp.sum(ocean_cells * centred * centred, axis=(1, 2)), "sp")
        variance = spread / ocean_count
        reciprocal = lax.rsqrt(variance + 1e-05)[:, None, None]
        whitened = centred * reciprocal
        normed = (whitened * gain_rows + shift_rows).astype(jnp.bfloat16)
        back_now = (ocean_cells * cotangent[batch_index].astype(jnp.float32)).astype(jnp.bfloat16)
        pixel_in, pixel_back = (
            lax.all_to_all(
                normed.reshape(channels, height * breadth),
                "lvl",
                split_axis=1,
                concat_axis=0,
                tiled=True,
            ),
            lax.all_to_all(
                back_now.reshape(channels, height * breadth),
                "lvl",
                split_axis=1,
                concat_axis=0,
                tiled=True,
            ),
        )
        hidden = (
            jnp.einsum("ch,cp->hp", expand_all, pixel_in, preferred_element_type=jnp.float32)
            + uplift_wide
        )
        active, slope_fn = jax.vjp(jax.nn.gelu, hidden)
        active_low = active.astype(jnp.bfloat16)
        result = (
            jnp.einsum("hc,hp->cp", shrink_all, active_low, preferred_element_type=jnp.float32)
            + offset_wide
        ).astype(jnp.bfloat16)
        grad_active = jnp.einsum(
            "hc,cp->hp", shrink_all, pixel_back, preferred_element_type=jnp.float32
        )
        grad_hidden = slope_fn(grad_active)[0].astype(jnp.bfloat16)
        grad_normed = jnp.einsum(
            "ch,hp->cp", expand_all, grad_hidden, preferred_element_type=jnp.float32
        ).astype(jnp.bfloat16)
        full_expand = full_expand + jnp.einsum(
            "cp,hp->ch", pixel_in, grad_hidden, preferred_element_type=jnp.float32
        )
        full_uplift = full_uplift + jnp.sum(grad_hidden.astype(jnp.float32), axis=1)
        full_shrink = full_shrink + jnp.einsum(
            "hp,cp->hc", active_low, pixel_back, preferred_element_type=jnp.float32
        )
        full_offset = full_offset + jnp.sum(pixel_back.astype(jnp.float32), axis=1)
        result_chan, grad_chan = (
            lax.all_to_all(result, "lvl", split_axis=0, concat_axis=1, tiled=True),
            lax.all_to_all(grad_normed, "lvl", split_axis=0, concat_axis=1, tiled=True),
        )
        mixed_back = result_chan.reshape(channels, height, breadth).astype(jnp.float32)
        outputs.append(ocean_cells * (field_now.astype(jnp.float32) + mixed_back))
        grad_norm = grad_chan.reshape(channels, height, breadth).astype(jnp.float32)
        plain_sum, cross_sum = lax.psum(
            (jnp.sum(grad_norm, axis=(1, 2)), jnp.sum(grad_norm * whitened, axis=(1, 2))), "sp"
        )
        gain_grad = gain_grad + cross_sum
        shift_grad = shift_grad + plain_sum
        grad_conv = reciprocal * (
            gain_rows * grad_norm
            - ocean_cells
            * gain_rows
            * (plain_sum[:, None, None] + whitened * cross_sum[:, None, None])
            / ocean_count
        )
        kernel_local = kernel_local + kernel_terms(grad_conv, framed, height, breadth)
        rimmed = extended(grad_conv, (("sp", 1),), margin)
        rimmed = jnp.pad(rimmed, ((0, 0), (0, 0), (margin, margin)))
        input_grads.append(
            valid_rows
            * (back_now.astype(jnp.float32) + depthwise_back(rimmed, kernel, height, breadth))
        )
    share_expand, share_uplift, share_shrink, share_offset = (
        lax.psum_scatter(full_expand, "sp", scatter_dimension=1, tiled=True),
        lax.psum_scatter(full_uplift, "sp", scatter_dimension=0, tiled=True),
        lax.psum_scatter(full_shrink, "sp", scatter_dimension=0, tiled=True),
        lax.psum_scatter(full_offset, "sp", scatter_dimension=0, tiled=True),
    )
    share_expand, share_uplift, share_shrink, share_offset = lax.psum(
        (share_expand, share_uplift, share_shrink, share_offset), "lvl"
    )
    kernel_grad = lax.psum(kernel_local, "sp")
    scales_grad = jnp.stack([gain_grad, shift_grad], axis=0)
    step_float = (step_count + 1).astype(jnp.float32)
    kernel_moment, kernel_next = adamw(
        kernel, kernel_first, kernel_second, kernel_grad, 0.15, step_float
    )
    scales_moment, scales_next = adamw(
        scales, scales_first, scales_second, scales_grad, 0.2, step_float
    )
    expand_moment, expand_next = adamw(
        expand, expand_first, expand_second, share_expand, 0.035, step_float
    )
    uplift_moment, uplift_next = adamw(
        uplift, uplift_first, uplift_second, share_uplift, 0.1, step_float
    )
    shrink_moment, shrink_next = adamw(
        shrink, shrink_first, shrink_second, share_shrink, 0.018, step_float
    )
    offset_moment, offset_next = adamw(
        offset, offset_first, offset_second, share_offset, 0.1, step_float
    )
    return (
        jnp.stack(outputs, axis=0),
        jnp.stack(input_grads, axis=0),
        kernel_grad,
        kernel_moment,
        kernel_next,
        scales_grad,
        scales_moment,
        scales_next,
        share_expand,
        expand_moment,
        expand_next,
        share_uplift,
        uplift_moment,
        uplift_next,
        share_shrink,
        shrink_moment,
        shrink_next,
        share_offset,
        offset_moment,
        offset_next,
        step_count + 1,
    )


def solution(mesh):
    in_specs = (
        P(None, "lvl", "sp", None),
        P(None, "lvl", "sp", None),
        P(None, "sp", None),
        P(None, "sp"),
        P(),
        P("lvl", None),
        P("lvl", None),
        P("lvl", None),
        P(None, "lvl"),
        P(None, "lvl"),
        P(None, "lvl"),
        P(None, "sp"),
        P(None, "sp"),
        P(None, "sp"),
        P("sp"),
        P("sp"),
        P("sp"),
        P("sp", None),
        P("sp", None),
        P("sp", None),
        P("sp"),
        P("sp"),
        P("sp"),
    )
    out_specs = (
        P(None, "lvl", "sp", None),
        P(None, "lvl", "sp", None),
        P("lvl", None),
        P("lvl", None),
        P("lvl", None),
        P(None, "lvl"),
        P(None, "lvl"),
        P(None, "lvl"),
        P(None, "sp"),
        P(None, "sp"),
        P(None, "sp"),
        P("sp"),
        P("sp"),
        P("sp"),
        P("sp", None),
        P("sp", None),
        P("sp", None),
        P("sp"),
        P("sp"),
        P("sp"),
        P(),
    )
    return jax.shard_map(
        on_device, mesh=mesh, in_specs=in_specs, out_specs=out_specs, check_vma=False
    )
```

profile of v0, /device:TPU:30, one launch (start us, length us, event | category | flops | bytes accessed | tf_op | source)
XLA Modules:
  0.0 1194.6 jit_solution(14420484921146090667)
XLA Ops:
  38.5 37.3 %multiply_reduce_fusion.151 = (f32[200]{0:T(256)}, f32[200,16,128]{2,1,0:T(8,128)}) fusion(f32[16,128]{1,0:T(8,128)S(1)} %bitcast.437, f32[200]{0:T(256)} %bitcast.735, f32[200]{0:T(256)} %bitcast.567, f32[200]{0:T(256)} %bitcast.573, f32[200,22,128]{2,1,0:T(8,128)S(1)} %maximum_convert_fusion.1, f32[200]{0:T(256)} %bitcast.579, f32[200]{0:T(256)} %bitcast.585, ...), kind=kLoop, calls=%fused_computation.734 | loop fusion | flops 40550200 | bytes 15615680 | tf_op jit(solution)/shard_map/reduce_sum | solution.py:145
  78.0 3.7 maximum_convert_fusion
  82.1 32.7 %multiply_reduce_fusion.150 = (f32[200]{0:T(256)S(1)}, f32[200,16,128]{2,1,0:T(8,128)}) fusion(f32[16,128]{1,0:T(8,128)S(1)} %bitcast.432, f32[200]{0:T(256)S(1)} %bitcast.738, f32[200]{0:T(256)S(1)} %bitcast.568, f32[200]{0:T(256)S(1)} %bitcast.574, f32[200,22,128]{2,1,0:T(8,128)S(1)} %maximum_convert_fusion.2, f32[200]{0:T(256)S(1)} %bitcast.580, ...), kind=kLoop, calls=%fused_computation.729 | loop fusion | flops 40550200 | bytes 15623968 | tf_op jit(solution)/shard_map/reduce_sum | solution.py:145
  115.0 67.8 %multiply_reduce_fusion.152 = (f32[200]{0:T(256)S(1)}, f32[200,16,128]{2,1,0:T(8,128)}) fusion(f32[16,128]{1,0:T(8,128)S(1)} %bitcast.442, f32[200]{0:T(256)S(1)} %bitcast.739, f32[200]{0:T(256)S(1)} %bitcast.569, f32[200]{0:T(256)S(1)} %bitcast.575, f32[200,22,128]{2,1,0:T(8,128)} %maximum_convert_fusion, f32[200]{0:T(256)S(1)} %bitcast.581, ...), kind=kLoop, calls=%fused_computation.739 | loop fusion | flops 40550200 | bytes 15612992 | tf_op jit(solution)/shard_map/reduce_sum | solution.py:145
  182.8 13.0 %all-reduce.13 = (f32[200]{0:T(256)S(1)}, f32[]{:T(128)}, f32[200]{0:T(256)S(1)}, f32[]{:T(128)}, f32[200]{0:T(256)S(1)}, /*index=5*/f32[]{:T(128)}) all-reduce(f32[200]{0:T(256)S(1)} %get-tuple-element.218, f32[]{:T(128)} %get-tuple-element.290, f32[200]{0:T(256)S(1)} %copy-done.197, ...), channel_id=1, replica_groups=mesh['lvl'=4,'sp'=8] {'sp'}, use_global_device_ids=true, to_apply=%region_13.14 | all-reduce | flops 603 | bytes 4824 | tf_op jit(solution)/shard_map/psum | solution.py:144
  205.5 12.5 %all-reduce.12 = (f32[200]{0:T(256)S(1)}, f32[200]{0:T(256)S(1)}, f32[200]{0:T(256)S(1)}) all-reduce(f32[200]{0:T(256)S(1)} %fusion.45, f32[200]{0:T(256)S(1)} %fusion.44, f32[200]{0:T(256)S(1)} %fusion.43), channel_id=1, replica_groups=mesh['lvl'=4,'sp'=8] {'sp'}, use_global_device_ids=true, to_apply=%region_17.18 | all-reduce | flops 600 | bytes 4800 | tf_op jit(solution)/shard_map/psum | solution.py:150
  218.2 5.4 add_convert_fusion.5
  226.4 5.1 all-to-all-start.2
  237.8 11.6 all-to-all-done.2
  249.4 6.5 all-to-all-start.8
  259.5 23.5 %all-reduce.16 = (bf16[800]{0:T(1024)(128)(2,1)S(1)}, bf16[3200]{0:T(1024)(128)(2,1)S(1)}) all-reduce(bf16[800]{0:T(1024)(128)(2,1)S(1)} %dynamic-update-slice.1, bf16[3200]{0:T(1024)(128)(2,1)S(1)} %dynamic-update-slice), channel_id=1, replica_groups=mesh['lvl'=4,'sp'=8] {'sp'}, use_global_device_ids=true, to_apply=%add.7 | all-reduce | flops 4000 | bytes 16000
  290.2 9.4 convolution_add_fusion.1
  299.6 5.1 all-to-all-start
  304.7 10.6 convert_reduce_fusion.1
  315.3 6.3 all-to-all-done
  321.6 6.1 all-to-all-start.6
  327.8 10.3 fusion.268
  338.0 5.8 convolution_add_fusion.2
  345.7 5.8 all-to-all-start.4
  351.5 10.7 convert_reduce_fusion.2
  362.2 7.3 all-to-all-done.4
  369.5 5.8 all-to-all-start.10
  375.5 8.1 fusion.267
  383.6 8.4 convolution_add_fusion
  393.2 9.5 convert_reduce_fusion
  404.4 12.1 %add_add_fusion.1 = f32[800,3200]{0,1:T(8,128)} fusion(f32[800,3200]{0,1:T(8,128)} %fusion.267, f32[800,3200]{0,1:T(8,128)} %fusion.268, bf16[800,512]{1,0:T(8,128)(2,1)S(1)} %bitcast.425, bf16[3200,512]{0,1:T(8,128)(2,1)S(1)} %get-tuple-element.305), kind=kOutput, calls=%fused_computation.127 | convolution fusion | flops 2626560000 | bytes 34816000 | tf_op jit(solution)/shard_map/cp,hp->ch/dot_general | solution.py:189
  421.0 7.5 convolution_convert_fusion.1
  428.6 6.4 all-to-all-start.9
  435.4 12.6 %fusion.241 = f32[3200,800]{1,0:T(8,128)} fusion(bf16[800,512]{1,0:T(8,128)(2,1)} %bitcast.90, f32[512,3200]{1,0:T(8,128)} %convolution_add_fusion.1), kind=kOutput, calls=%fused_computation.791 | convolution fusion | flops 2636185600 | bytes 17612800 | tf_op jit(solution)/shard_map/hp,cp->hc/dot_general | solution.py:193
  448.0 11.6 fusion.238
  459.6 19.6 %add_add_fusion = f32[3200,800]{1,0:T(8,128)} fusion(f32[3200,800]{1,0:T(8,128)} %fusion.238, f32[3200,800]{1,0:T(8,128)} %fusion.241, bf16[800,512]{1,0:T(8,128)(2,1)S(1)} %bitcast.423, f32[512,3200]{1,0:T(8,128)} %convolution_add_fusion), kind=kOutput, calls=%fused_computation.126 | convolution fusion | flops 2641305600 | bytes 38092800 | tf_op jit(solution)/shard_map/hp,cp->hc/dot_general | solution.py:193
  479.2 9.1 add_convert_fusion.2
  488.3 6.6 convolution_convert_fusion.2
  494.9 9.0 add_convert_fusion
  503.9 5.1 all-to-all-start.7
  509.0 7.5 convolution_convert_fusion
  516.5 11.1 add_convert_fusion.4
  527.6 6.9 all-to-all-start.11
  552.5 6.5 all-to-all-start.3
  570.9 13.1 %all-reduce.11 = (f32[200]{0:T(256)}, f32[200]{0:T(256)}, f32[200]{0:T(256)S(1)}, f32[200]{0:T(256)S(1)}, f32[200]{0:T(256)S(1)}, /*index=5*/f32[200]{0:T(256)S(1)}) all-reduce(f32[200]{0:T(256)S(1)} %multiply_reduce_fusion.147, f32[200]{0:T(256)S(1)} %convert_reduce_fusion.3, ...), channel_id=1, replica_groups=mesh['lvl'=4,'sp'=8] {'sp'}, use_global_device_ids=true, to_apply=%region_29.30 | all-reduce | flops 1200 | bytes 9600 | tf_op jit(solution)/shard_map/psum | solution.py:204
  584.0 19.0 %multiply_reduce_fusion.98 = (f32[200]{0:T(256)S(1)}, f32[200]{0:T(256)S(1)}, f32[200]{0:T(256)S(1)}, f32[200]{0:T(256)S(1)}, f32[200]{0:T(256)S(1)}, /*index=5*...) fusion(f32[200,22,128]{2,1,0:T(8,128)S(1)} %copy-done.2, ...), kind=kLoop, calls=%fused_computation.668 | loop fusion | flops 18838000 | bytes 12315716 | tf_op jit(solution)/shard_map/reduce_sum | solution.py:77
  611.0 5.1 all-to-all-start.5
  616.1 19.0 %multiply_reduce_fusion.49 = (f32[200]{0:T(256)S(1)}, f32[200]{0:T(256)S(1)}, f32[200]{0:T(256)S(1)}, f32[200]{0:T(256)S(1)}, f32[200]{0:T(256)S(1)}, /*index=5*...) fusion(f32[200,22,128]{2,1,0:T(8,128)S(1)} %copy-done.5, ...), kind=kLoop, calls=%fused_computation.619 | loop fusion | flops 18838000 | bytes 12315716 | tf_op jit(solution)/shard_map/reduce_sum | solution.py:77
  639.4 3.6 collective-permute-start.9
  643.1 5.1 all-to-all-start.1
  648.2 19.3 %multiply_reduce_fusion = (f32[200]{0:T(256)S(1)}, f32[200]{0:T(256)S(1)}, f32[200]{0:T(256)S(1)}, f32[200]{0:T(256)S(1)}, f32[200]{0:T(256)S(1)}, /*index=5*/f3...) fusion(f32[200,22,128]{2,1,0:T(8,128)S(1)} %copy-done.1, ...), kind=kLoop, calls=%fused_computation.570 | loop fusion | flops 18838000 | bytes 12315268 | tf_op jit(solution)/shard_map/reduce_sum | solution.py:77
  688.9 21.1 %multiply_reduce_fusion.85 = (f32[200]{0:T(256)S(1)}, f32[200]{0:T(256)S(1)}, f32[200]{0:T(256)S(1)}, f32[200]{0:T(256)S(1)}, f32[200]{0:T(256)S(1)}, /*index=5*...) fusion(f32[200,16,128]{2,1,0:T(8,128)} %copy-done.13, ...), kind=kLoop, calls=%fused_computation.655 | loop fusion | flops 10647000 | bytes 7383200 | tf_op jit(solution)/shard_map/reduce_sum | solution.py:77
  710.0 17.9 %multiply_reduce_fusion.50 = (f32[200]{0:T(256)S(1)}, f32[200]{0:T(256)S(1)}, f32[200]{0:T(256)S(1)}, f32[200]{0:T(256)S(1)}, f32[200]{0:T(256)S(1)}, /*index=5*...) fusion(f32[200,16,128]{2,1,0:T(8,128)S(1)} %copy-done.14, ...), kind=kLoop, calls=%fused_computation.620 | loop fusion | flops 14742000 | bytes 7387200 | tf_op jit(solution)/shard_map/reduce_sum | solution.py:77
  728.1 20.6 %multiply_reduce_fusion.134 = (f32[200]{0:T(256)S(1)}, f32[200]{0:T(256)S(1)}, f32[200]{0:T(256)S(1)}, f32[200]{0:T(256)S(1)}, f32[200]{0:T(256)S(1)}, /*index=5...) fusion(f32[200,16,128]{2,1,0:T(8,128)} %copy-done.7, ...), kind=kLoop, calls=%fused_computation.704 | loop fusion | flops 10647000 | bytes 7383200 | tf_op jit(solution)/shard_map/reduce_sum | solution.py:77
  748.7 17.7 %multiply_reduce_fusion.99 = (f32[200]{0:T(256)S(1)}, f32[200]{0:T(256)S(1)}, f32[200]{0:T(256)S(1)}, f32[200]{0:T(256)S(1)}, f32[200]{0:T(256)S(1)}, /*index=5*...) fusion(f32[200,16,128]{2,1,0:T(8,128)S(1)} %copy-done.8, ...), kind=kLoop, calls=%fused_computation.669 | loop fusion | flops 14742000 | bytes 7387200 | tf_op jit(solution)/shard_map/reduce_sum | solution.py:77
  766.5 12.3 %multiply_reduce_fusion.36 = (f32[200]{0:T(256)S(1)}, f32[200]{0:T(256)S(1)}, f32[200]{0:T(256)S(1)}, f32[200]{0:T(256)S(1)}, f32[200]{0:T(256)S(1)}, /*index=5*...) fusion(f32[200,16,128]{2,1,0:T(8,128)} %copy-done.10, ...), kind=kLoop, calls=%fused_computation.606 | loop fusion | flops 10647000 | bytes 7383200 | tf_op jit(solution)/shard_map/reduce_sum | solution.py:77
  779.1 17.5 %multiply_reduce_fusion.1 = (f32[200]{0:T(256)S(1)}, f32[200]{0:T(256)S(1)}, f32[200]{0:T(256)S(1)}, f32[200]{0:T(256)S(1)}, f32[200]{0:T(256)S(1)}, /*index=5*/...) fusion(f32[200,16,128]{2,1,0:T(8,128)S(1)} %copy-done.11, ...), kind=kLoop, calls=%fused_computation.571 | loop fusion | flops 14742000 | bytes 7387200 | tf_op jit(solution)/shard_map/reduce_sum | solution.py:77
  796.7 27.7 %all-reduce.10 = (f32[200,49]{0,1:T(8,128)S(1)}, f32[3200]{0:T(1024)S(1)}, f32[800]{0:T(1024)S(1)}) all-reduce(f32[200,49]{0,1:T(8,128)S(1)} %add_add_fusion.3, f32[3200]{0:T(1024)S(1)} %add_add_fusion.4, f32[800]{0:T(1024)S(1)} %add.1578), channel_id=1, replica_groups=mesh['lvl'=4,'sp'=8] {'sp'}, use_global_device_ids=true, to_apply=%region_177.178 | all-reduce | flops 13800 | bytes 110400 | tf_op jit(solution)/shard_map/psum | solution.py:232
  824.6 8.3 all-reduce.14
  834.9 3.9 add_multiply_fusion.2
  844.1 5.2 select_maximum_fusion.4
  849.3 5.3 select_maximum_fusion.2
  855.8 5.1 select_maximum_fusion
  861.2 99.3 %fusion.229 = f32[1,200,16,128]{3,2,1,0:T(8,128)} fusion(f32[200,22,134]{2,1,0:T(8,128)} %select_maximum_fusion.4, f32[200,16,128]{2,1,0:T(8,128)S(1)} %copy-done.9, f32[200,3,128]{2,1,0:T(4,128)} %collective-permute-done.6, f32[200,3,128]{2,1,0:T(4,128)} %collective-permute-done.7, f32[16,128]{1,0:T(8,128)S(1)} %bitcast.446, f32[200]{0:T(256)} %bitcast.736, ...), kind=kLoop, calls=%fused_computation.741 | loop fusion | flops 44646400 | bytes 73570656 | tf_op jit(solution)/shard_map/stack | solution.py:255
  960.5 101.0 %fusion.230 = f32[1,200,16,128]{3,2,1,0:T(8,128)} fusion(f32[200,22,134]{2,1,0:T(8,128)} %select_maximum_fusion.2, f32[200,16,128]{2,1,0:T(8,128)} %copy-done.13, f32[200,3,128]{2,1,0:T(4,128)} %collective-permute-done.8, f32[200,3,128]{2,1,0:T(4,128)} %collective-permute-done.9, f32[16,128]{1,0:T(8,128)S(1)} %bitcast.441, f32[16]{0:T(128)S(1)} %copy-done.177, ...), kind=kLoop, calls=%fused_computation.742 | loop fusion | flops 44646400 | bytes 73570656 | tf_op jit(solution)/shard_map/stack | solution.py:255
  1062.2 98.7 %fusion.231 = f32[1,200,16,128]{3,2,1,0:T(8,128)} fusion(f32[200,22,134]{2,1,0:T(8,128)} %select_maximum_fusion, f32[200,16,128]{2,1,0:T(8,128)S(1)} %copy-done.12, f32[200,3,128]{2,1,0:T(4,128)} %collective-permute-done.10, f32[200,3,128]{2,1,0:T(4,128)} %copy-done.43, f32[16,128]{1,0:T(8,128)S(1)} %bitcast.436, f32[16]{0:T(128)S(1)} %copy-done.174, ...), kind=kLoop, calls=%fused_computation.743 | loop fusion | flops 44646400 | bytes 73570656 | tf_op jit(solution)/shard_map/stack | solution.py:255
  1160.9 4.6 pad_maximum_fusion.1
  1165.5 10.3 all-reduce.19.cloned.1.call-done
  1175.8 5.0 multiply_subtract_fusion
  (577 shorter events, 145.3 us)
Async XLA Ops:
  7.2 283.0 %all-gather.3.cloned.1.call-start = ((), (), s32[]{:S(2)}) async-start(), calls=%async_computation.14 | async-start | bytes 6451200 | tf_op jit(solution)/shard_map/all_gather | solution.py:117
  9.7 295.0 %all-gather.5.cloned.1.call-start = ((), (), s32[]{:S(2)}) async-start(), calls=%async_computation.15 | async-start | bytes 6451200 | tf_op jit(solution)/shard_map/all_gather | solution.py:119
  13.2 19.7 %collective-permute-start.2 = (bf16[200,3,128]{2,1,0:T(4,128)(2,1)S(1)}, bf16[200,3,128]{2,1,0:T(4,128)(2,1)S(1)}, u32[]{:S(2)}, u32[]{:S(2)}) collective-permute-start(bf16[200,3,128]{2,1,0:T(4,128)(2,1)S(1)} %get-tuple-element.237), channel_id=1, source_target_pairs={{0,1},{1,2},{2,3},{3,4},{4,5},{5,6},{6,7},{8,9},{9,10},{10,11},{11... | collective-permute-start | bytes 460808 | tf_op jit(solution)/shard_map/ppermute | solution.py:23
  15.4 21.1 %collective-permute-start.3 = (bf16[200,3,128]{2,1,0:T(4,128)(2,1)S(1)}, bf16[200,3,128]{2,1,0:T(4,128)(2,1)}, u32[]{:S(2)}, u32[]{:S(2)}) collective-permute-start(bf16[200,3,128]{2,1,0:T(4,128)(2,1)S(1)} %get-tuple-element.238), channel_id=1, source_target_pairs={{1,0},{2,1},{3,2},{4,3},{5,4},{6,5},{7,6},{9,8},{10,9},{11,10},{12... | collective-permute-start | bytes 460808 | tf_op jit(solution)/shard_map/ppermute | solution.py:25
  19.9 55.8 %collective-permute-start.4 = (bf16[200,3,128]{2,1,0:T(4,128)(2,1)}, bf16[200,3,128]{2,1,0:T(4,128)(2,1)S(1)}, u32[]{:S(2)}, u32[]{:S(2)}) collective-permute-start(bf16[200,3,128]{2,1,0:T(4,128)(2,1)} %get-tuple-element.239), channel_id=1, source_target_pairs={{0,1},{1,2},{2,3},{3,4},{4,5},{5,6},{6,7},{8,9},{9,10},{10,11},{11... | collective-permute-start | bytes 460808 | tf_op jit(solution)/shard_map/ppermute | solution.py:23
  21.8 53.9 %collective-permute-start.5 = (bf16[200,3,128]{2,1,0:T(4,128)(2,1)}, bf16[200,3,128]{2,1,0:T(4,128)(2,1)}, u32[]{:S(2)}, u32[]{:S(2)}) collective-permute-start(bf16[200,3,128]{2,1,0:T(4,128)(2,1)} %get-tuple-element.240), channel_id=1, source_target_pairs={{1,0},{2,1},{3,2},{4,3},{5,4},{6,5},{7,6},{9,8},{10,9},{11,10},{12... | collective-permute-start | bytes 460808 | tf_op jit(solution)/shard_map/ppermute | solution.py:25
  26.4 51.6 %collective-permute-start = (bf16[200,3,128]{2,1,0:T(4,128)(2,1)}, bf16[200,3,128]{2,1,0:T(4,128)(2,1)}, u32[]{:S(2)}, u32[]{:S(2)}) collective-permute-start(bf16[200,3,128]{2,1,0:T(4,128)(2,1)} %get-tuple-element.235), channel_id=1, source_target_pairs={{0,1},{1,2},{2,3},{3,4},{4,5},{5,6},{6,7},{8,9},{9,10},{10,11},{11... | collective-permute-start | bytes 460808 | tf_op jit(solution)/shard_map/ppermute | solution.py:23
  30.1 84.7 %copy-start.59 = (f32[200,1]{0,1:T(1,128)}, f32[200,1]{0,1:T(1,128)S(1)}, u32[]{:S(2)}) copy-start(f32[200,1]{0,1:T(1,128)S(1)} %get-tuple-element.260) | copy-start | bytes 2404
  30.1 84.7 %copy-start.61 = (f32[200,1]{0,1:T(1,128)}, f32[200,1]{0,1:T(1,128)S(1)}, u32[]{:S(2)}) copy-start(f32[200,1]{0,1:T(1,128)S(1)} %get-tuple-element.261) | copy-start | bytes 2404
  30.1 84.7 %copy-start.63 = (f32[200,1]{0,1:T(1,128)}, f32[200,1]{0,1:T(1,128)S(1)}, u32[]{:S(2)}) copy-start(f32[200,1]{0,1:T(1,128)S(1)} %get-tuple-element.262) | copy-start | bytes 2404
  30.1 84.7 %copy-start.65 = (f32[200,1]{0,1:T(1,128)}, f32[200,1]{0,1:T(1,128)S(1)}, u32[]{:S(2)}) copy-start(f32[200,1]{0,1:T(1,128)S(1)} %get-tuple-element.263) | copy-start | bytes 2404
  30.2 84.7 %copy-start.67 = (f32[200,1]{0,1:T(1,128)}, f32[200,1]{0,1:T(1,128)S(1)}, u32[]{:S(2)}) copy-start(f32[200,1]{0,1:T(1,128)S(1)} %get-tuple-element.264) | copy-start | bytes 2404
  30.2 84.7 %copy-start.69 = (f32[200,1]{0,1:T(1,128)}, f32[200,1]{0,1:T(1,128)S(1)}, u32[]{:S(2)}) copy-start(f32[200,1]{0,1:T(1,128)S(1)} %get-tuple-element.265) | copy-start | bytes 2404
  30.2 84.7 %copy-start.71 = (f32[200,1]{0,1:T(1,128)}, f32[200,1]{0,1:T(1,128)S(1)}, u32[]{:S(2)}) copy-start(f32[200,1]{0,1:T(1,128)S(1)} %get-tuple-element.266) | copy-start | bytes 2404
  30.2 84.7 %copy-start.73 = (f32[200,1]{0,1:T(1,128)}, f32[200,1]{0,1:T(1,128)S(1)}, u32[]{:S(2)}) copy-start(f32[200,1]{0,1:T(1,128)S(1)} %get-tuple-element.267) | copy-start | bytes 2404
  30.2 84.7 %copy-start.75 = (f32[200,1]{0,1:T(1,128)}, f32[200,1]{0,1:T(1,128)S(1)}, u32[]{:S(2)}) copy-start(f32[200,1]{0,1:T(1,128)S(1)} %get-tuple-element.268) | copy-start | bytes 2404
  30.2 84.7 %copy-start.77 = (f32[200,1]{0,1:T(1,128)}, f32[200,1]{0,1:T(1,128)S(1)}, u32[]{:S(2)}) copy-start(f32[200,1]{0,1:T(1,128)S(1)} %get-tuple-element.269) | copy-start | bytes 2404
  30.2 84.7 %copy-start.79 = (f32[200,1]{0,1:T(1,128)}, f32[200,1]{0,1:T(1,128)S(1)}, u32[]{:S(2)}) copy-start(f32[200,1]{0,1:T(1,128)S(1)} %get-tuple-element.270) | copy-start | bytes 2404
  30.2 84.7 %copy-start.81 = (f32[200,1]{0,1:T(1,128)}, f32[200,1]{0,1:T(1,128)S(1)}, u32[]{:S(2)}) copy-start(f32[200,1]{0,1:T(1,128)S(1)} %get-tuple-element.271) | copy-start | bytes 2404
  32.3 199.3 %copy-start.49 = (f32[1,16,128]{2,1,0:T(8,128)}, f32[1,16,128]{2,1,0:T(8,128)S(1)}, u32[]{:S(2)}) copy-start(f32[1,16,128]{2,1,0:T(8,128)S(1)} %get-tuple-element.293) | copy-start | bytes 24580
  32.3 199.3 %copy-start.51 = (f32[1,16,128]{2,1,0:T(8,128)}, f32[1,16,128]{2,1,0:T(8,128)S(1)}, u32[]{:S(2)}) copy-start(f32[1,16,128]{2,1,0:T(8,128)S(1)} %get-tuple-element.209) | copy-start | bytes 24580
  32.3 224.9 %copy-start.47 = (f32[1,16,128]{2,1,0:T(8,128)}, f32[1,16,128]{2,1,0:T(8,128)S(1)}, u32[]{:S(2)}) copy-start(f32[1,16,128]{2,1,0:T(8,128)S(1)} %get-tuple-element.291) | copy-start | bytes 24580
  32.8 45.2 %collective-permute-start.1 = (bf16[200,3,128]{2,1,0:T(4,128)(2,1)}, bf16[200,3,128]{2,1,0:T(4,128)(2,1)}, u32[]{:S(2)}, u32[]{:S(2)}) collective-permute-start(bf16[200,3,128]{2,1,0:T(4,128)(2,1)} %get-tuple-element.236), channel_id=1, source_target_pairs={{1,0},{2,1},{3,2},{4,3},{5,4},{6,5},{7,6},{9,8},{10,9},{11,10},{12... | collective-permute-start | bytes 460808 | tf_op jit(solution)/shard_map/ppermute | solution.py:25
  114.9 67.8 %copy-start.197 = (f32[200]{0:T(256)S(1)}, f32[200]{0:T(256)}, u32[]{:S(2)}) copy-start(f32[200]{0:T(256)} %get-tuple-element.214) | copy-start | bytes 2404
  226.4 23.0 %all-to-all-start.2 = ((bf16[200,4,512]{2,0,1:T(8,128)(2,1)}), bf16[200,4,512]{2,0,1:T(8,128)(2,1)}, u32[]{:S(2)}, u32[]{:S(2)}) async-start(bf16[200,4,512]{2,0,1:T(8,128)(2,1)} %copy.85), calls=%async_computation.2 | async-start | bytes 1638400 | tf_op jit(solution)/shard_map/all_to_all | solution.py:157
  249.4 50.2 %all-to-all-start.8 = ((bf16[200,4,512]{2,0,1:T(8,128)(2,1)}), bf16[200,4,512]{2,0,1:T(8,128)(2,1)}, u32[]{:S(2)}, u32[]{:S(2)}) async-start(bf16[200,4,512]{2,0,1:T(8,128)(2,1)} %copy.91), calls=%async_computation.8 | async-start | bytes 1638400 | tf_op jit(solution)/shard_map/all_to_all | solution.py:164
  299.6 22.0 %all-to-all-start = ((bf16[200,4,512]{2,0,1:T(8,128)(2,1)}), bf16[200,4,512]{2,0,1:T(8,128)(2,1)S(1)}, u32[]{:S(2)}, u32[]{:S(2)}) async-start(bf16[200,4,512]{2,0,1:T(8,128)(2,1)} %copy.83), calls=%async_computation | async-start | bytes 1638400 | tf_op jit(solution)/shard_map/all_to_all | solution.py:157
  321.6 24.1 %all-to-all-start.6 = ((bf16[200,4,512]{2,0,1:T(8,128)(2,1)}), bf16[200,4,512]{2,0,1:T(8,128)(2,1)S(1)}, u32[]{:S(2)}, u32[]{:S(2)}) async-start(bf16[200,4,512]{2,0,1:T(8,128)(2,1)} %copy.89), calls=%async_computation.6 | async-start | bytes 1638400 | tf_op jit(solution)/shard_map/all_to_all | solution.py:164
  345.7 23.8 %all-to-all-start.4 = ((bf16[200,4,512]{2,0,1:T(8,128)(2,1)}), bf16[200,4,512]{2,0,1:T(8,128)(2,1)S(1)}, u32[]{:S(2)}, u32[]{:S(2)}) async-start(bf16[200,4,512]{2,0,1:T(8,128)(2,1)} %copy.87), calls=%async_computation.4 | async-start | bytes 1638400 | tf_op jit(solution)/shard_map/all_to_all | solution.py:157
  369.5 23.8 %all-to-all-start.10 = ((bf16[200,4,512]{2,0,1:T(8,128)(2,1)}), bf16[200,4,512]{2,0,1:T(8,128)(2,1)S(1)}, u32[]{:S(2)}, u32[]{:S(2)}) async-start(bf16[200,4,512]{2,0,1:T(8,128)(2,1)} %copy.93), calls=%async_computation.10 | async-start | bytes 1638400 | tf_op jit(solution)/shard_map/all_to_all | solution.py:164
  375.3 686.3 %reduce-scatter.3.cloned.1.call-start = ((), (), s32[]{:S(2)}) async-start(), calls=%async_computation.16 | async-start | bytes 12902400 | tf_op jit(solution)/shard_map/reduce_scatter | solution.py:224
  428.6 75.3 %all-to-all-start.9 = ((bf16[4,200,512]{2,1,0:T(8,128)(2,1)}), bf16[4,200,512]{2,1,0:T(8,128)(2,1)S(1)}, u32[]{:S(2)}, u32[]{:S(2)}) async-start(bf16[4,200,512]{2,1,0:T(8,128)(2,1)} %bitcast.93), calls=%async_computation.9 | async-start | bytes 1638400 | tf_op jit(solution)/shard_map/all_to_all | solution.py:199
  435.0 626.6 %reduce-scatter.5.cloned.1.call-start = ((), (), s32[]{:S(2)}) async-start(), calls=%async_computation.17 | async-start | bytes 12902400 | tf_op jit(solution)/shard_map/reduce_scatter | solution.py:226
  503.9 23.7 %all-to-all-start.7 = ((bf16[4,200,512]{2,1,0:T(8,128)(2,1)}), bf16[4,200,512]{2,1,0:T(8,128)(2,1)S(1)}, u32[]{:S(2)}, u32[]{:S(2)}) async-start(bf16[4,200,512]{2,1,0:T(8,128)(2,1)} %bitcast.85), calls=%async_computation.7 | async-start | bytes 1638400 | tf_op jit(solution)/shard_map/all_to_all | solution.py:199
  527.6 24.9 %all-to-all-start.11 = ((bf16[4,200,512]{2,1,0:T(8,128)(2,1)}), bf16[4,200,512]{2,1,0:T(8,128)(2,1)}, u32[]{:S(2)}, u32[]{:S(2)}) async-start(bf16[4,200,512]{2,1,0:T(8,128)(2,1)} %bitcast.101), calls=%async_computation.11 | async-start | bytes 1638400 | tf_op jit(solution)/shard_map/all_to_all | solution.py:199
  552.5 58.5 %all-to-all-start.3 = ((bf16[4,200,512]{2,1,0:T(8,128)(2,1)}), bf16[4,200,512]{2,1,0:T(8,128)(2,1)}, u32[]{:S(2)}, u32[]{:S(2)}) async-start(bf16[4,200,512]{2,1,0:T(8,128)(2,1)} %bitcast.69), calls=%async_computation.3 | async-start | bytes 1638400 | tf_op jit(solution)/shard_map/all_to_all | solution.py:198
  605.3 236.7 %collective-permute-start.6 = (f32[200,3,128]{2,1,0:T(4,128)}, f32[200,3,128]{2,1,0:T(4,128)}, u32[]{:S(2)}, u32[]{:S(2)}) collective-permute-start(f32[200,3,128]{2,1,0:T(4,128)} %get-tuple-element.229), channel_id=1, source_target_pairs={{0,1},{1,2},{2,3},{3,4},{4,5},{5,6},{6,7},{8,9},{9,10},{10,11},{11... | collective-permute-start | bytes 921608 | tf_op jit(solution)/shard_map/ppermute | solution.py:23
  607.4 236.7 %collective-permute-start.7 = (f32[200,3,128]{2,1,0:T(4,128)}, f32[200,3,128]{2,1,0:T(4,128)}, u32[]{:S(2)}, u32[]{:S(2)}) collective-permute-start(f32[200,3,128]{2,1,0:T(4,128)} %get-tuple-element.230), channel_id=1, source_target_pairs={{1,0},{2,1},{3,2},{4,3},{5,4},{6,5},{7,6},{9,8},{10,9},{11,10},{12... | collective-permute-start | bytes 921608 | tf_op jit(solution)/shard_map/ppermute | solution.py:25
  611.0 32.1 %all-to-all-start.5 = ((bf16[4,200,512]{2,1,0:T(8,128)(2,1)}), bf16[4,200,512]{2,1,0:T(8,128)(2,1)S(1)}, u32[]{:S(2)}, u32[]{:S(2)}) async-start(bf16[4,200,512]{2,1,0:T(8,128)(2,1)} %bitcast.429), calls=%async_computation.5 | async-start | bytes 1638400 | tf_op jit(solution)/shard_map/all_to_all | solution.py:198
  637.4 211.9 %collective-permute-start.8 = (f32[200,3,128]{2,1,0:T(4,128)}, f32[200,3,128]{2,1,0:T(4,128)}, u32[]{:S(2)}, u32[]{:S(2)}) collective-permute-start(f32[200,3,128]{2,1,0:T(4,128)} %get-tuple-element.231), channel_id=1, source_target_pairs={{0,1},{1,2},{2,3},{3,4},{4,5},{5,6},{6,7},{8,9},{9,10},{10,11},{11... | collective-permute-start | bytes 921608 | tf_op jit(solution)/shard_map/ppermute | solution.py:23
  639.4 209.9 %collective-permute-start.9 = (f32[200,3,128]{2,1,0:T(4,128)}, f32[200,3,128]{2,1,0:T(4,128)}, u32[]{:S(2)}, u32[]{:S(2)}) collective-permute-start(f32[200,3,128]{2,1,0:T(4,128)} %get-tuple-element.232), channel_id=1, source_target_pairs={{1,0},{2,1},{3,2},{4,3},{5,4},{6,5},{7,6},{9,8},{10,9},{11,10},{12... | collective-permute-start | bytes 921608 | tf_op jit(solution)/shard_map/ppermute | solution.py:25
  643.1 39.4 %all-to-all-start.1 = ((bf16[4,200,512]{2,1,0:T(8,128)(2,1)}), bf16[4,200,512]{2,1,0:T(8,128)(2,1)}, u32[]{:S(2)}, u32[]{:S(2)}) async-start(bf16[4,200,512]{2,1,0:T(8,128)(2,1)} %bitcast.428), calls=%async_computation.1 | async-start | bytes 1638400 | tf_op jit(solution)/shard_map/all_to_all | solution.py:198
  648.2 527.6 %all-reduce.19.cloned.1.call-start = ((), (), s32[]{:S(2)}) async-start(), calls=%async_computation.18 | async-start | bytes 5734400 | tf_op jit(solution)/shard_map/psum | solution.py:229
  668.7 186.3 %collective-permute-start.10 = (f32[200,3,128]{2,1,0:T(4,128)}, f32[200,3,128]{2,1,0:T(4,128)}, u32[]{:S(2)}, u32[]{:S(2)}) collective-permute-start(f32[200,3,128]{2,1,0:T(4,128)} %get-tuple-element.233), channel_id=1, source_target_pairs={{0,1},{1,2},{2,3},{3,4},{4,5},{5,6},{6,7},{8,9},{9,10},{10,11},{11... | collective-permute-start | bytes 921608 | tf_op jit(solution)/shard_map/ppermute | solution.py:23
  778.8 54.0 %copy-start.191 = (f32[200]{0:T(256)S(1)}, f32[200]{0:T(256)}, u32[]{:S(2)}) copy-start(f32[200]{0:T(256)} %get-tuple-element.171) | copy-start | bytes 2404
  778.9 54.0 %copy-start.193 = (f32[200]{0:T(256)S(1)}, f32[200]{0:T(256)}, u32[]{:S(2)}) copy-start(f32[200]{0:T(256)} %copy-done.192) | copy-start | bytes 2404
  778.9 54.0 %copy-start.195 = (f32[200]{0:T(256)S(1)}, f32[200]{0:T(256)}, u32[]{:S(2)}) copy-start(f32[200]{0:T(256)} %copy-done.194) | copy-start | bytes 2404
  778.9 54.0 %copy-start.186 = (f32[200]{0:T(256)S(1)}, f32[200]{0:T(256)}, u32[]{:S(2)}) copy-start(f32[200]{0:T(256)} %get-tuple-element.172) | copy-start | bytes 2404
  778.9 54.0 %copy-start.188 = (f32[200]{0:T(256)S(1)}, f32[200]{0:T(256)}, u32[]{:S(2)}) copy-start(f32[200]{0:T(256)} %copy-done.187) | copy-start | bytes 2404
  778.9 54.0 %copy-start.190 = (f32[200]{0:T(256)S(1)}, f32[200]{0:T(256)}, u32[]{:S(2)}) copy-start(f32[200]{0:T(256)} %copy-done.189) | copy-start | bytes 2404
  778.9 54.0 %copy-start.181 = (f32[400]{0:T(512)S(1)}, f32[400]{0:T(512)}, u32[]{:S(2)}) copy-start(f32[400]{0:T(512)} %param.37) | copy-start | bytes 4804
  778.9 54.0 %copy-start.201 = (f32[400]{0:T(512)S(1)}, f32[400]{0:T(512)}, u32[]{:S(2)}) copy-start(f32[400]{0:T(512)} %param.38) | copy-start | bytes 4804
  778.9 54.0 %copy-start.202 = (f32[400]{0:T(512)S(1)}, f32[400]{0:T(512)}, u32[]{:S(2)}) copy-start(f32[400]{0:T(512)} %param.39) | copy-start | bytes 4804
  778.9 54.6 %copy-start.179 = (f32[2,200]{1,0:T(2,128)S(1)}, f32[2,200]{1,0:T(2,128)}, u32[]{:S(2)}) copy-start(f32[2,200]{1,0:T(2,128)} %param.31) | copy-start | bytes 4804
  779.0 54.6 %copy-start.198 = (f32[2,200]{1,0:T(2,128)S(1)}, f32[2,200]{1,0:T(2,128)}, u32[]{:S(2)}) copy-start(f32[2,200]{1,0:T(2,128)} %param.32) | copy-start | bytes 4804
  779.0 54.6 %copy-start.199 = (f32[2,200]{1,0:T(2,128)S(1)}, f32[2,200]{1,0:T(2,128)}, u32[]{:S(2)}) copy-start(f32[2,200]{1,0:T(2,128)} %param.33) | copy-start | bytes 4804
  779.0 55.2 %copy-start.55 = (f32[200,49]{0,1:T(8,128)S(1)}, f32[200,49]{0,1:T(8,128)}, u32[]{:S(2)}) copy-start(f32[200,49]{0,1:T(8,128)} %param.28) | copy-start | bytes 117604
  779.0 55.2 %copy-start.56 = (f32[200,49]{0,1:T(8,128)S(1)}, f32[200,49]{0,1:T(8,128)}, u32[]{:S(2)}) copy-start(f32[200,49]{0,1:T(8,128)} %param.29) | copy-start | bytes 117604
  779.0 55.2 %copy-start.57 = (f32[200,49]{0,1:T(8,128)S(1)}, f32[200,49]{0,1:T(8,128)}, u32[]{:S(2)}) copy-start(f32[200,49]{0,1:T(8,128)} %param.30) | copy-start | bytes 117604
  779.0 55.9 %copy-start.174 = (f32[16]{0:T(128)S(1)}, f32[16]{0:T(128)}, u32[]{:S(2)}) copy-start(f32[16]{0:T(128)} %copy-done.172) | copy-start | bytes 196
  779.0 55.9 %copy-start.177 = (f32[16]{0:T(128)S(1)}, f32[16]{0:T(128)}, u32[]{:S(2)}) copy-start(f32[16]{0:T(128)} %copy-done.175) | copy-start | bytes 196
  779.0 55.9 %copy-start.184 = (f32[16]{0:T(128)S(1)}, f32[16]{0:T(128)}, u32[]{:S(2)}) copy-start(f32[16]{0:T(128)} %copy-done.182) | copy-start | bytes 196
  842.0 13.0 %collective-permute-start.11 = (f32[200,3,128]{2,1,0:T(4,128)S(1)}, f32[200,3,128]{2,1,0:T(4,128)S(1)}, u32[]{:S(2)}, u32[]{:S(2)}) collective-permute-start(f32[200,3,128]{2,1,0:T(4,128)S(1)} %copy-done.46), channel_id=1, source_target_pairs={{1,0},{2,1},{3,2},{4,3},{5,4},{6,5},{7,6},{9,8},{10,9},{11,10},{12... | collective-permute-start | bytes 921608 | tf_op jit(solution)/shard_map/ppermute | solution.py:25
  1062.2 98.7 %copy-start.32 = (f32[1,200,16,128]{3,2,1,0:T(8,128)S(1)}, f32[1,200,16,128]{3,2,1,0:T(8,128)}, u32[]{:S(2)}) copy-start(f32[1,200,16,128]{3,2,1,0:T(8,128)} %fusion.229) | copy-start | bytes 4915204
  (177 other events, 1212.8 us)
Sparse Core Ops, SparseCore 0:
  9.9 50.3 all-gather.2
  62.2 43.3 all-gather.4
  416.7 89.0 reduce-scatter.2
  509.2 86.6 reduce-scatter.4
  1061.7 114.0 all-reduce.18
where the time goes:
time: 1210 us; the launch traced here: 1190 us
  other arithmetic  687 us (57%)
  matrix products  179 us (15%)
  starting transfers between devices  103 us (9%)
  blocking collectives  98.1 us (8%)
  local copies, waits for them, and re-layouts  63.1 us (5%)
  waiting for transfers between devices  40.6 us (3%)
  between operations  23.8 us (2%)
    another operation x4, other arithmetic, on_device(): jnp.stack(input_grads, axis=0)  304 us
    reduce_sum x9, other arithmetic, kernel_terms(): jnp.sum(grad_conv * framed[:, vertical:vertical + height, lateral:lateral...  164 us
    reduce_sum x3, other arithmetic, on_device(): jnp.sum(ocean_cells * convolved, axis=(1, 2))  138 us
    dot_general x3, matrix products, on_device(): jnp.einsum('hp,cp->hc', active_low, pixel_back, preferred_element_type=jn...  43.8 us
    dot_general x3, matrix products, on_device(): jnp.einsum('hc,cp->hp', shrink_all, pixel_back, preferred_element_type=jn...  30.8 us
    dot_general x3, matrix products, on_device(): jnp.einsum('cp,hp->ch', pixel_in, grad_hidden, preferred_element_type=jnp...  30.5 us
    dot_general x3, matrix products, on_device(): jnp.einsum('hc,hp->cp', shrink_all, active_low, preferred_element_type=jn...  29.1 us
    psum x1, blocking collectives, on_device(): kernel_grad = lax.psum(kernel_local, 'sp')  27.7 us
  transfers between devices with their start and end apart: 29, of which 7 were waited for; matrix products, arithmetic and copies ran while one was open for 74% of the time, Pallas kernels for 0%

commit v1 on v0

v1 whole, which is shorter than its diff:
```python
import functools
import math

import jax
import jax.numpy as jnp
from jax import lax
from jax.experimental import pallas as pl
from jax.experimental.pallas import tpu as pltpu
from jax.sharding import PartitionSpec as P

KW = 7
MARGIN = KW // 2
GROUP = 8
ROWS = 16

beta_one = 0.9
beta_two = 0.999
epsilon = 1e-08
weight_decay = 0.01
GELU_A = math.sqrt(2.0 / math.pi)
GELU_B = 0.044715


def adamw(weight, first, second, grad, rate, step_float):
    first_new = beta_one * first + (1.0 - beta_one) * grad
    second_new = beta_two * second + (1.0 - beta_two) * grad * grad
    fix_first = 1.0 - jnp.power(beta_one, step_float)
    fix_second = 1.0 - jnp.power(beta_two, step_float)
    update = (
        first_new / fix_first / (jnp.sqrt(second_new / fix_second) + epsilon)
        + weight_decay * weight
    )
    return (second_new, weight - rate * update)


def lane_tap_masks(width):
    lane = lax.broadcasted_iota(jnp.int32, (GROUP, width), 1)
    return [
        jnp.logical_and(lane + (b - MARGIN) >= 0, lane + (b - MARGIN) < width)
        for b in range(KW)
    ]


def shifted(value, amount):
    width = value.shape[-1]
    turn = (-amount) % width
    return value if turn == 0 else pltpu.roll(value, turn, 1)


def put_columns(columns):
    lane = lax.broadcasted_iota(jnp.int32, (GROUP, 128), 1)
    out = jnp.zeros((GROUP, 128), jnp.float32)
    for at, column in columns:
        out = jnp.where(lane == at, column, out)
    return out


def conv_body(
    crop, x_ref, cot_ref, up_ref, dn_ref, k_ref, mask_ref,
    conv_ref, xt_ref, dres_ref, stat_ref, scr, scc, wscr,
):
    batches, _, height, width = x_ref.shape
    masks = lane_tap_masks(width)
    for a in range(KW):
        for b in range(KW):
            t = a * KW + b
            spread = jnp.broadcast_to(k_ref[:, t : t + 1], (GROUP, width))
            wscr[t] = jnp.where(masks[b], spread, 0.0)

    def one(m, stats):
        for c in range(GROUP):
            scr[c * height : (c + 1) * height, :] = x_ref[m, c].astype(jnp.float32)
            scc[c * height : (c + 1) * height, :] = cot_ref[m, c].astype(jnp.float32)
        limit = crop[m, 0]
        for i in range(height):
            row = scr[pl.ds(i, GROUP, stride=height), :]
            xt_ref[m, MARGIN + i] = jnp.where(i < limit, row, 0.0)
            back = scc[pl.ds(i, GROUP, stride=height), :]
            dres_ref[m, i] = (back * mask_ref[m, i : i + 1, :]).astype(jnp.bfloat16)
        for r in range(MARGIN):
            xt_ref[m, r] = up_ref[m, r].astype(jnp.float32)
            xt_ref[m, MARGIN + height + r] = dn_ref[m, r].astype(jnp.float32)
        total = jnp.zeros((GROUP, width), jnp.float32)
        for base in range(0, height, ROWS):
            acc = [None] * ROWS
            for b in range(KW):
                rolled = [
                    shifted(xt_ref[m, base + r], b - MARGIN) for r in range(ROWS + KW - 1)
                ]
                for a in range(KW):
                    tap = wscr[a * KW + b]
                    for i in range(ROWS):
                        term = tap * rolled[i + a]
                        acc[i] = term if acc[i] is None else acc[i] + term
            for i in range(ROWS):
                conv_ref[m, base + i] = acc[i]
                total = total + acc[i] * mask_ref[m, base + i : base + i + 1, :]
        cells = jnp.sum(mask_ref[m])
        summed = jnp.sum(total, axis=1, keepdims=True)
        mean = summed / jnp.maximum(cells, 1.0)
        spread = jnp.zeros((GROUP, width), jnp.float32)
        for i in range(height):
            off = conv_ref[m, i] - mean
            spread = spread + off * off * mask_ref[m, i : i + 1, :]
        squares = jnp.sum(spread, axis=1, keepdims=True)
        lane = lax.broadcasted_iota(jnp.int32, (GROUP, 128), 1)
        stats = jnp.where(lane == m, summed, stats)
        stats = jnp.where(lane == batches + m, squares, stats)
        return jnp.where(lane == 2 * batches + m, cells, stats)

    stat_ref[...] = lax.fori_loop(0, batches, one, jnp.zeros((GROUP, 128), jnp.float32))


def conv_forward(crop, x, cot, up, down, kernel, mask_cells):
    batches, channels, height, width = x.shape
    groups = pl.cdiv(channels, GROUP)
    natural = pl.BlockSpec((batches, GROUP, height, width), lambda g, c: (0, g, 0, 0))
    turned = lambda rows: pl.BlockSpec((batches, rows, GROUP, width), lambda g, c: (0, 0, g, 0))
    return pl.pallas_call(
        conv_body,
        grid_spec=pltpu.PrefetchScalarGridSpec(
            num_scalar_prefetch=1,
            grid=(groups,),
            in_specs=[
                natural,
                natural,
                turned(MARGIN),
                turned(MARGIN),
                pl.BlockSpec((GROUP, KW * KW), lambda g, c: (g, 0)),
                pl.BlockSpec((batches, height, width), lambda g, c: (0, 0, 0)),
            ],
            out_specs=[
                turned(height),
                turned(height + 2 * MARGIN),
                turned(height),
                pl.BlockSpec((GROUP, 128), lambda g, c: (g, 0)),
            ],
            scratch_shapes=[
                pltpu.VMEM((GROUP * height, width), jnp.float32),
                pltpu.VMEM((GROUP * height, width), jnp.float32),
                pltpu.VMEM((KW * KW, GROUP, width), jnp.float32),
            ],
        ),
        out_shape=[
            jax.ShapeDtypeStruct((batches, height, channels, width), jnp.float32),
            jax.ShapeDtypeStruct((batches, height + 2 * MARGIN, channels, width), jnp.float32),
            jax.ShapeDtypeStruct((batches, height, channels, width), jnp.bfloat16),
            jax.ShapeDtypeStruct((channels, 128), jnp.float32),
        ],
        cost_estimate=pl.CostEstimate(
            flops=2 * KW * KW * batches * channels * height * width,
            bytes_accessed=30 * batches * channels * height * width,
            transcendentals=0,
        ),
    )(crop, x, cot, up, down, kernel, mask_cells)


def chunks_of(total, size):
    return [(start, min(size, total - start)) for start in range(0, total, size)]


def nt(a, b):
    return lax.dot_general(a, b, (((1,), (1,)), ((), ())), preferred_element_type=jnp.float32)


def nn(a, b):
    return jnp.dot(a, b, preferred_element_type=jnp.float32)


def mlp_body(
    pin_ref, back_ref, et_ref, w_ref, up_ref, off_ref,
    res_ref, dn_ref, ge_out, gw_out, gu_out, go_out,
    pin, pint, back, backt, res_acc, dn_acc, ge, gw, gu, go,
):
    m = pl.program_id(0)
    last = pl.num_programs(0) - 1
    rows, channels, width = pin_ref.shape[1:]
    hidden = et_ref.shape[0]
    for r in range(rows):
        cols = slice(r * width, (r + 1) * width)
        value = pin_ref[0, r]
        pin[:, cols] = value
        pint[cols, :] = value.T
        value = back_ref[0, r]
        back[:, cols] = value
        backt[cols, :] = value.T

    @pl.when(m == 0)
    def _():
        ge[...] = jnp.zeros_like(ge)
        gw[...] = jnp.zeros_like(gw)
        gu[...] = jnp.zeros_like(gu)
        go[...] = jnp.zeros_like(go)

    go[...] += jnp.sum(backt[...].astype(jnp.float32), axis=0, keepdims=True)
    for index, (start, size) in enumerate(chunks_of(hidden, 512)):
        span = slice(start, start + size)
        et = et_ref[span, :]
        wt = w_ref[span, :]
        hid = nt(pint[...], et) + up_ref[:, span]
        dact = nt(backt[...], wt)
        square = hid * hid
        inner = GELU_A * hid * (1.0 + GELU_B * square)
        t = jnp.tanh(inner)
        half = 0.5 * (1.0 + t)
        act = (hid * half).astype(jnp.bfloat16)
        slope = half + 0.5 * hid * (1.0 - t * t) * (GELU_A * (1.0 + 3.0 * GELU_B * square))
        dhid = (slope * dact).astype(jnp.bfloat16)
        res_part = nn(act, wt)
        dn_part = nn(dhid, et)
        if index == 0:
            res_acc[...] = res_part
            dn_acc[...] = dn_part
        else:
            res_acc[...] += res_part
            dn_acc[...] += dn_part
        ge[:, span] += nn(pin[...], dhid)
        gw[:, span] += nn(back[...], act)
        gu[:, span] += jnp.sum(dhid.astype(jnp.float32), axis=0, keepdims=True)

        @pl.when(m == last)
        def _():
            ge_out[span, :] = ge[:, span].astype(jnp.bfloat16).T
            gw_out[span, :] = gw[:, span].astype(jnp.bfloat16).T

    for r in range(rows):
        cols = slice(r * width, (r + 1) * width)
        res_ref[0, r] = (res_acc[cols, :] + off_ref[...]).astype(jnp.bfloat16).T
        dn_ref[0, r] = dn_acc[cols, :].astype(jnp.bfloat16).T

    @pl.when(m == last)
    def _():
        gu_out[...] = gu[...]
        go_out[...] = go[...]


def mlp(pin, back, expand_t, shrink, uplift, offset):
    batches, rows, channels, width = pin.shape
    hidden = expand_t.shape[0]
    pixels = rows * width
    block = pl.BlockSpec((1, rows, channels, width), lambda m: (m, 0, 0, 0))
    whole = lambda shape: pl.BlockSpec(shape, lambda m: (0, 0), pipeline_mode=pl.Buffered(1))
    bf, f32 = jnp.bfloat16, jnp.float32
    return pl.pallas_call(
        mlp_body,
        grid=(batches,),
        in_specs=[
            block, block,
            whole((hidden, channels)), whole((hidden, channels)),
            whole((1, hidden)), whole((1, channels)),
        ],
        out_specs=[
            block, block,
            whole((hidden, channels)), whole((hidden, channels)),
            whole((1, hidden)), whole((1, channels)),
        ],
        out_shape=[
            jax.ShapeDtypeStruct(pin.shape, bf),
            jax.ShapeDtypeStruct(pin.shape, bf),
            jax.ShapeDtypeStruct((hidden, channels), bf),
            jax.ShapeDtypeStruct((hidden, channels), bf),
            jax.ShapeDtypeStruct((1, hidden), f32),
            jax.ShapeDtypeStruct((1, channels), f32),
        ],
        scratch_shapes=[
            pltpu.VMEM((channels, pixels), bf),
            pltpu.VMEM((pixels, channels), bf),
            pltpu.VMEM((channels, pixels), bf),
            pltpu.VMEM((pixels, channels), bf),
            pltpu.VMEM((pixels, channels), f32),
            pltpu.VMEM((pixels, channels), f32),
            pltpu.VMEM((channels, hidden), f32),
            pltpu.VMEM((channels, hidden), f32),
            pltpu.VMEM((1, hidden), f32),
            pltpu.VMEM((1, channels), f32),
        ],
        compiler_params=pltpu.CompilerParams(vmem_limit_bytes=62 * 1024 * 1024),
        cost_estimate=pl.CostEstimate(
            flops=12 * batches * pixels * channels * hidden,
            bytes_accessed=2 * 4 * channels * hidden,
            transcendentals=batches * pixels * hidden,
        ),
    )(pin, back, expand_t, shrink, uplift, offset)


def sums_body(xt_ref, res_ref, dn_ref, conv_ref, mask_ref, par_ref, out_ref, stat_ref, scr):
    batches, height = res_ref.shape[:2]
    width = res_ref.shape[3]

    def one(m, stats):
        lane = lax.broadcasted_iota(jnp.int32, (GROUP, 128), 1)
        mean = jnp.sum(jnp.where(lane == m, par_ref[...], 0.0), axis=1, keepdims=True)
        rho = jnp.sum(jnp.where(lane == batches + m, par_ref[...], 0.0), axis=1, keepdims=True)
        mean = jnp.broadcast_to(mean, (GROUP, width))
        rho = jnp.broadcast_to(rho, (GROUP, width))
        plain = jnp.zeros((GROUP, width), jnp.float32)
        cross = jnp.zeros((GROUP, width), jnp.float32)
        for i in range(height):
            grad = dn_ref[m, i].astype(jnp.float32)
            plain = plain + grad
            cross = cross + grad * ((conv_ref[m, i] - mean) * rho)
            value = xt_ref[m, MARGIN + i] + res_ref[m, i].astype(jnp.float32)
            scr[pl.ds(i, GROUP, stride=height), :] = value * mask_ref[m, i : i + 1, :]
        for c in range(GROUP):
            out_ref[m, c] = scr[c * height : (c + 1) * height, :]
        stats = jnp.where(lane == m, jnp.sum(plain, axis=1, keepdims=True), stats)
        return jnp.where(lane == batches + m, jnp.sum(cross, axis=1, keepdims=True), stats)

    stat_ref[...] = lax.fori_loop(0, batches, one, jnp.zeros((GROUP, 128), jnp.float32))


def output_and_sums(xt, res, dn, conv, mask_cells, params):
    batches, height, channels, width = res.shape
    turned = lambda rows: pl.BlockSpec((batches, rows, GROUP, width), lambda g: (0, 0, g, 0))
    return pl.pallas_call(
        sums_body,
        grid=(pl.cdiv(channels, GROUP),),
        in_specs=[
            turned(height + 2 * MARGIN),
            turned(height), turned(height), turned(height),
            pl.BlockSpec((batches, height, width), lambda g: (0, 0, 0)),
            pl.BlockSpec((GROUP, 128), lambda g: (g, 0)),
        ],
        out_specs=[
            pl.BlockSpec((batches, GROUP, height, width), lambda g: (0, g, 0, 0)),
            pl.BlockSpec((GROUP, 128), lambda g: (g, 0)),
        ],
        out_shape=[
            jax.ShapeDtypeStruct((batches, channels, height, width), jnp.float32),
            jax.ShapeDtypeStruct((channels, 128), jnp.float32),
        ],
        scratch_shapes=[pltpu.VMEM((GROUP * height, width), jnp.float32)],
        cost_estimate=pl.CostEstimate(
            flops=10 * batches * channels * height * width,
            bytes_accessed=20 * batches * channels * height * width,
            transcendentals=0,
        ),
    )(xt, res, dn, conv, mask_cells, params)


def conv_back_body(
    crop, xt_ref, grad_ref, up_ref, dn_ref, cot_ref, k_ref, mask_ref,
    out_ref, kg_ref, scr, wscr, frame, sums,
):
    batches, height = grad_ref.shape[:2]
    width = grad_ref.shape[3]
    masks = lane_tap_masks(width)
    for a in range(KW):
        for b in range(KW):
            t = a * KW + b
            spread = jnp.broadcast_to(k_ref[:, t : t + 1], (GROUP, width))
            wscr[t] = jnp.where(masks[KW - 1 - b], spread, 0.0)
            sums[t] = jnp.zeros((GROUP, width), jnp.float32)

    def one(m, carry):
        for r in range(MARGIN):
            frame[r] = up_ref[m, r]
            frame[MARGIN + height + r] = dn_ref[m, r]
        for i in range(height):
            frame[MARGIN + i] = grad_ref[m, i]
        for base in range(0, height, ROWS):
            for b in range(KW):
                rolled = [
                    shifted(xt_ref[m, base + r], b - MARGIN) for r in range(ROWS + KW - 1)
                ]
                for a in range(KW):
                    part = None
                    for i in range(ROWS):
                        term = frame[MARGIN + base + i] * rolled[i + a]
                        part = term if part is None else part + term
                    sums[a * KW + b] += part
            acc = [None] * ROWS
            for b in range(KW):
                rolled = [
                    shifted(frame[base + r], MARGIN - b) for r in range(ROWS + KW - 1)
                ]
                for a in range(KW):
                    tap = wscr[a * KW + b]
                    for i in range(ROWS):
                        term = tap * rolled[i + KW - 1 - a]
                        acc[i] = term if acc[i] is None else acc[i] + term
            for i in range(ROWS):
                scr[pl.ds(base + i, GROUP, stride=height), :] = acc[i]
        row = lax.broadcasted_iota(jnp.int32, (height, width), 0)
        for c in range(GROUP):
            dres = cot_ref[m, c].astype(jnp.float32) * mask_ref[m]
            total = dres + scr[c * height : (c + 1) * height, :]
            out_ref[m, c] = jnp.where(row < crop[m, 0], total, 0.0)
        return carry

    lax.fori_loop(0, batches, one, 0)
    columns = []
    for t in range(KW * KW):
        kept = jnp.where(masks[t % KW], sums[t], 0.0)
        columns.append((t, jnp.sum(kept, axis=1, keepdims=True)))
    kg_ref[...] = put_columns(columns)


def conv_backward(crop, xt, grad_conv, up, down, cot, kernel, mask_cells):
    batches, height, channels, width = grad_conv.shape
    natural = pl.BlockSpec((batches, GROUP, height, width), lambda g, c: (0, g, 0, 0))
    turned = lambda rows: pl.BlockSpec((batches, rows, GROUP, width), lambda g, c: (0, 0, g, 0))
    return pl.pallas_call(
        conv_back_body,
        grid_spec=pltpu.PrefetchScalarGridSpec(
            num_scalar_prefetch=1,
            grid=(pl.cdiv(channels, GROUP),),
            in_specs=[
                turned(height + 2 * MARGIN),
                turned(height),
                turned(MARGIN), turned(MARGIN),
                natural,
                pl.BlockSpec((GROUP, KW * KW), lambda g, c: (g, 0)),
                pl.BlockSpec((batches, height, width), lambda g, c: (0, 0, 0)),
            ],
            out_specs=[natural, pl.BlockSpec((GROUP, 128), lambda g, c: (g, 0))],
            scratch_shapes=[
                pltpu.VMEM((GROUP * height, width), jnp.float32),
                pltpu.VMEM((KW * KW, GROUP, width), jnp.float32),
                pltpu.VMEM((height + 2 * MARGIN, GROUP, width), jnp.float32),
                pltpu.VMEM((KW * KW, GROUP, width), jnp.float32),
            ],
        ),
        out_shape=[
            jax.ShapeDtypeStruct((batches, channels, height, width), jnp.float32),
            jax.ShapeDtypeStruct((channels, 128), jnp.float32),
        ],
        cost_estimate=pl.CostEstimate(
            flops=4 * KW * KW * batches * channels * height * width,
            bytes_accessed=14 * batches * channels * height * width,
            transcendentals=0,
        ),
    )(crop, xt, grad_conv, up, down, cot, kernel, mask_cells)


def neighbours(head, tail, axis):
    count = lax.axis_size(axis)
    up = lax.ppermute(tail, axis, [(i, i + 1) for i in range(count - 1)])
    down = lax.ppermute(head, axis, [(i + 1, i) for i in range(count - 1)])
    return up, down


def on_device(
    input_field, cotangent, ocean_mask, crop_rows, step_count,
    kernel, kernel_first, kernel_second,
    scales, scales_first, scales_second,
    expand, expand_first, expand_second,
    uplift, uplift_first, uplift_second,
    shrink, shrink_first, shrink_second,
    offset, offset_first, offset_second,
):
    f32, bf = jnp.float32, jnp.bfloat16
    batches, channels, height, width = input_field.shape
    sp = lax.axis_size("sp")
    lvl = lax.axis_size("lvl")
    expand_all = lax.all_gather(expand.T.astype(bf), "sp", axis=0, tiled=True)
    shrink_all = lax.all_gather(shrink.astype(bf), "sp", axis=0, tiled=True)
    uplift_all = lax.all_gather(uplift.astype(bf), "sp", axis=0, tiled=True)
    offset_all = lax.all_gather(offset.astype(bf), "sp", axis=0, tiled=True)

    valid = (jnp.arange(height, dtype=jnp.int32)[None, :] < crop_rows).astype(f32)
    mask_cells = ocean_mask.astype(f32) * valid[:, :, None]
    valid_low = valid.astype(bf)[:, None, :, None]
    head = input_field[:, :, :MARGIN] * valid_low[:, :, :MARGIN]
    tail = input_field[:, :, height - MARGIN :] * valid_low[:, :, height - MARGIN :]
    up, down = neighbours(head.transpose(0, 2, 1, 3), tail.transpose(0, 2, 1, 3), "sp")
    conv, xt, dres, stats = conv_forward(
        crop_rows, input_field, cotangent, up, down, kernel, mask_cells
    )
    every = lax.all_gather(stats[:, : 4 * batches], "sp", axis=0)
    sums = every[:, :, :batches]
    squares = every[:, :, batches : 2 * batches]
    cells = every[:, :, 2 * batches : 3 * batches]
    count = jnp.maximum(jnp.sum(cells, axis=0), 1.0)
    mean = jnp.sum(sums, axis=0) / count
    gap = sums / jnp.maximum(cells, 1.0) - mean[None]
    variance = jnp.sum(squares + cells * gap * gap, axis=0) / count
    rho = lax.rsqrt(variance + 1e-05)

    def spread(stat):
        return stat.T[:, None, :, None]

    gain = scales[0][None, None, :, None]
    shift = scales[1][None, None, :, None]
    normed = ((conv - spread(mean)) * spread(rho) * gain + shift).astype(bf)

    def to_pixels(v):
        return lax.all_to_all(v, "lvl", split_axis=1, concat_axis=2, tiled=True)

    def to_channels(v):
        return lax.all_to_all(v, "lvl", split_axis=2, concat_axis=1, tiled=True)

    pixel_back = to_pixels(dres)
    pixel_in = to_pixels(normed)
    result, grad_normed, grad_expand, grad_shrink, grad_uplift, grad_offset = mlp(
        pixel_in, pixel_back, expand_all, shrink_all,
        uplift_all.astype(f32)[None], offset_all.astype(f32)[None],
    )
    result = to_channels(result)
    grad_normed = to_channels(grad_normed)
    params = jnp.concatenate([mean, rho], axis=1)
    params = jnp.pad(params, ((0, 0), (0, 128 - params.shape[1])))
    block_output, local = output_and_sums(xt, result, grad_normed, conv, mask_cells, params)
    both = lax.psum(local[:, : 2 * batches], "sp")
    plain, cross = both[:, :batches], both[:, batches:]
    scales_grad = jnp.stack([jnp.sum(cross, axis=1), jnp.sum(plain, axis=1)], axis=0)
    whitened = (conv - spread(mean)) * spread(rho)
    grad_conv = spread(rho) * (
        gain * grad_normed.astype(f32)
        - mask_cells[:, :, None, :] * gain * (spread(plain) + whitened * spread(cross)) / spread(count)
    )
    back_up, back_down = neighbours(
        grad_conv[:, :MARGIN], grad_conv[:, height - MARGIN :], "sp"
    )
    input_grad, kernel_cols = conv_backward(
        crop_rows, xt, grad_conv, back_up, back_down, cotangent, kernel, mask_cells
    )
    kernel_grad = lax.psum(kernel_cols[:, : KW * KW], "sp")

    def own_share(partial):
        rows = partial.shape[0] // sp
        parts = lax.all_to_all(
            partial.reshape(sp, rows, partial.shape[1]), "sp", split_axis=0, concat_axis=0
        )
        share = jnp.sum(parts.astype(f32), axis=0).astype(bf)
        return jnp.sum(lax.all_gather(share, "lvl", axis=0).astype(f32), axis=0)

    share_expand = own_share(grad_expand)
    share_shrink = own_share(grad_shrink)
    small = lax.psum(
        jnp.concatenate([grad_uplift[0], grad_offset[0]]), ("sp", "lvl")
    )
    place = lax.axis_index("sp")
    share_uplift = lax.dynamic_slice_in_dim(small, place * uplift.shape[0], uplift.shape[0])
    share_offset = lax.dynamic_slice_in_dim(
        small, uplift_all.shape[0] + place * offset.shape[0], offset.shape[0]
    )
    step_float = (step_count + 1).astype(f32)
    kernel_moment, kernel_next = adamw(
        kernel, kernel_first, kernel_second, kernel_grad, 0.15, step_float
    )
    scales_moment, scales_next = adamw(
        scales, scales_first, scales_second, scales_grad, 0.2, step_float
    )
    expand_grad = share_expand.T
    expand_moment, expand_next = adamw(
        expand, expand_first, expand_second, expand_grad, 0.035, step_float
    )
    uplift_moment, uplift_next = adamw(
        uplift, uplift_first, uplift_second, share_uplift, 0.1, step_float
    )
    shrink_moment, shrink_next = adamw(
        shrink, shrink_first, shrink_second, share_shrink, 0.018, step_float
    )
    offset_moment, offset_next = adamw(
        offset, offset_first, offset_second, share_offset, 0.1, step_float
    )
    return (
        block_output, input_grad,
        kernel_grad, kernel_moment, kernel_next,
        scales_grad, scales_moment, scales_next,
        expand_grad, expand_moment, expand_next,
        share_uplift, uplift_moment, uplift_next,
        share_shrink, shrink_moment, shrink_next,
        share_offset, offset_moment, offset_next,
        step_count + 1,
    )


def solution(mesh):
    tile = P(None, "lvl", "sp", None)
    by_channel = P("lvl", None)
    by_scale = P(None, "lvl")
    by_hidden = P(None, "sp")
    by_row = P("sp", None)
    line = P("sp")
    in_specs = (
        tile, tile, P(None, "sp", None), P(None, "sp"), P(),
        by_channel, by_channel, by_channel,
        by_scale, by_scale, by_scale,
        by_hidden, by_hidden, by_hidden,
        line, line, line,
        by_row, by_row, by_row,
        line, line, line,
    )
    out_specs = (
        tile, tile,
        by_channel, by_channel, by_channel,
        by_scale, by_scale, by_scale,
        by_hidden, by_hidden, by_hidden,
        line, line, line,
        by_row, by_row, by_row,
        line, line, line,
        P(),
    )
    return jax.shard_map(
        on_device, mesh=mesh, in_specs=in_specs, out_specs=out_specs, check_vma=False
    )
```

time: 1210 us -> 851 us (0.70)
  other arithmetic: 687 us -> 34.5 us
  Pallas kernels: 0 us -> 220 us
  waiting for transfers between devices: 40.6 us -> 225 us
  matrix products: 179 us -> 0 us
  blocking collectives: 98.1 us -> 267 us
  starting transfers between devices: 103 us -> 37.2 us
  local copies, waits for them, and re-layouts: 63.1 us -> 37 us
    reduce_sum x25 -> x7, other arithmetic: 323 us -> 14.7 us  [the longest x2 9.04 us: own_share(): share = jnp.sum(parts.astype(f32), axis=0).astype(bf)]
    another operation x5 -> x0, other arithmetic: 306 us -> none  [the longest x4 304 us: on_device(): jnp.stack(input_grads, axis=0)]
    pallas_call x0 -> x4, Pallas kernels: none -> 220 us  [the longest x1 98.9 us: mlp(): pl.pallas_call(mlp_body, grid=(batches,), in_specs=[block, block, whole((...]
    all_to_all x12 -> x4, waiting for transfers between devices: 30.2 us -> 217 us  [the longest x1 84.2 us: to_channels(): return lax.all_to_all(v, 'lvl', split_axis=2, concat_axis=1, tiled=True)]
    dot_general x18 -> x0, matrix products: 179 us -> none  [the longest x3 43.8 us: on_device(): jnp.einsum('hp,cp->hc', active_low, pixel_back, preferred_element_type=jn...]
    all_to_all x0 -> x2, blocking collectives: none -> 126 us  [the longest x1 68 us: own_share(): lax.all_to_all(partial.reshape(sp, rows, partial.shape[1]), 'sp', split_a...]
    all_to_all x12 -> x4, starting transfers between devices: 69.6 us -> 25.8 us  [the longest x2 11.9 us: to_pixels(): return lax.all_to_all(v, 'lvl', split_axis=1, concat_axis=2, tiled=True)]
    convert_element_type x18 -> x1, local copies, waits for them, and re-layouts: 36.2 us -> 1.61 us  [on_device(): normed = ((conv - spread(mean)) * spread(rho) * gain + shift).astype(bf)]
  transfers between devices with their start and end apart: 29 -> 12, of which waited for: 7 -> 6; matrix products, arithmetic and copies ran while one was open for 74% -> 6% of each run, Pallas kernels for 0% -> 14%
where the time goes in v1:
time: 851 us; the launch traced here: 839 us
  blocking collectives  267 us (31%)
  waiting for transfers between devices  225 us (26%)
  Pallas kernels  220 us (26%)
  starting transfers between devices  37.2 us (4%)
  local copies, waits for them, and re-layouts  37 us (4%)
  other arithmetic  34.5 us (4%)
  between operations  17.6 us (2%)
    pallas_call x1, Pallas kernels, mlp(): pl.pallas_call(mlp_body, grid=(batches,), in_specs=[block, block, whole((...  98.9 us
    all_to_all x1, waiting for transfers between devices, to_channels(): return lax.all_to_all(v, 'lvl', split_axis=2, concat_axis=1, tiled=True)  84.2 us
    all_to_all x2, waiting for transfers between devices, to_pixels(): return lax.all_to_all(v, 'lvl', split_axis=1, concat_axis=2, tiled=True)  78 us
    all_to_all x1, blocking collectives, own_share(): lax.all_to_all(partial.reshape(sp, rows, partial.shape[1]), 'sp', split_a...  68 us
    psum x1, blocking collectives, on_device(): lax.psum(jnp.concatenate([grad_uplift[0], grad_offset[0]]), ('sp', 'lvl'))  62 us
    all_to_all x1, blocking collectives, to_channels(): return lax.all_to_all(v, 'lvl', split_axis=2, concat_axis=1, tiled=True)  57.9 us
    all_to_all x1, waiting for transfers between devices, own_share(): lax.all_to_all(partial.reshape(sp, rows, partial.shape[1]), 'sp', split_a...  54.4 us
    pallas_call x1, Pallas kernels, conv_backward(): pl.pallas_call(conv_back_body, grid_spec=pltpu.PrefetchScalarGridSpec(num...  51.5 us
  transfers between devices with their start and end apart: 12, of which 6 were waited for; matrix products, arithmetic and copies ran while one was open for 6% of the time, Pallas kernels for 14%

profile of v1, /device:TPU:30, one launch (start us, length us, event | category | flops | bytes accessed | tf_op | source)
XLA Modules:
  0.0 839.3 jit_solution(2907569340653028812)
XLA Ops:
  7.3 2.4 convert_bitcast_fusion
  9.9 0.5 fusion.17
  10.6 2.1 collective-permute-start
  12.8 3.8 collective-permute-start.1
  16.6 0.9 convert_element_type.74
  17.7 0.7 copy.118.crop
  18.3 0.7 copy.119.k_ref
  19.1 0.7 convert_multiply_fusion.mask_ref
  19.8 2.2 collective-permute-done.up_ref
  22.0 6.1 collective-permute-done.1.dn_ref
  28.1 0.8 copy-done.17
  28.9 46.6 %shard_map.385 = (f32[3,16,200,128]{3,2,1,0:T(8,128)}, f32[3,22,200,128]{3,2,1,0:T(8,128)}, bf16[3,16,200,128]{3,2,1,0:T(8,128)(2,1)}, f32[200,128]{1,0:T(8,128)}) custom-call(s32[3,1]{1,0:T(4,128)} %copy.118.crop, bf16[3,200,16,128]{3,2,1,0:T(8,128)(2,1)} %x_ref.1, bf16[3,200,16,128]{3,2,1,0:T(8,128)(2,1)} %cot_ref.3, bf16[3,3,200,128]{3,2,1,0:T(8,128)(2,1)} %copy-done.16, ...), custom_call_target="tpu_custom_call" | custom-call | flops 120422400 | bytes 36864000 | tf_op jit(solution)/shard_map/pallas_call | solution.py:119
  75.5 0.9 slice_bitcast_fusion
  76.5 13.0 %all-gather.3 = f32[8,200,12]{1,2,0:T(8,128)S(1)} all-gather(f32[1,200,12]{1,2,0:T(8,128)S(1)} %copy.120), channel_id=2, replica_groups=mesh['lvl'=4,'sp'=8] {'sp'}, dimensions={0}, use_global_device_ids=true | all-gather | bytes 86400 | tf_op jit(solution)/shard_map/all_gather | solution.py:470
  89.6 3.8 add_convert_fusion
  93.4 1.6 copy.121
  95.0 5.1 all-to-all-start
  100.1 3.4 copy.123
  103.5 50.7 %all-to-all-done = bf16[3,16,200,128]{3,2,0,1:T(8,128)(2,1)S(1)} async-done(((bf16[3,16,200,128]{3,2,0,1:T(8,128)(2,1)}), bf16[3,16,200,128]{3,2,0,1:T(8,128)(2,1)S(1)}, u32[]{:S(2)}, u32[]{:S(2)}) %all-to-all-start) | async-done | bytes 2457632 | tf_op jit(solution)/shard_map/all_to_all | solution.py:488
  154.2 6.8 all-to-all-start.1
  161.1 0.6 dynamic-slice
  163.4 20.8 %all-reduce.3 = (bf16[3200]{0:T(1024)(128)(2,1)S(1)}, bf16[800]{0:T(1024)(128)(2,1)S(1)}) all-reduce(bf16[3200]{0:T(1024)(128)(2,1)S(1)} %dynamic-update-slice, bf16[800]{0:T(1024)(128)(2,1)S(1)} %dynamic-update-slice.1), channel_id=1, replica_groups=mesh['lvl'=4,'sp'=8] {'sp'}, use_global_device_ids=true, to_apply=%add.1 | all-reduce | flops 4000 | bytes 16000
  184.2 0.6 reshape.130.up_ref
  184.8 0.6 reshape.131.off_ref
  185.4 1.6 copy.122
  187.1 27.3 %all-to-all-done.1 = bf16[3,16,200,128]{3,2,0,1:T(8,128)(2,1)} async-done(((bf16[3,16,200,128]{3,2,0,1:T(8,128)(2,1)}), bf16[3,16,200,128]{3,2,0,1:T(8,128)(2,1)}, u32[]{:S(2)}, u32[]{:S(2)}) %all-to-all-start.1) | async-done | bytes 2457632 | tf_op jit(solution)/shard_map/all_to_all | solution.py:488
  214.4 3.3 copy.124
  217.7 98.9 %shard_map.386 = (bf16[3,4,800,128]{3,2,1,0:T(8,128)(2,1)}, bf16[3,4,800,128]{3,2,1,0:T(8,128)(2,1)}, bf16[3200,800]{1,0:T(8,128)(2,1)}, bf16[3200,800]{1,0:T(8,...) custom-call(bf16[3,4,800,128]{3,2,1,0:T(8,128)(2,1)} %bitcast.71, bf16[3,4,800,128]{3,2,1,0:T(8,128)(2,1)} %bitcast.72, ...), custom_call_target="tpu_custom_call" | custom-call | flops 47185920000 | bytes 20480000 | tf_op jit(solution)/shard_map/pallas_call | solution.py:244
  316.6 3.1 copy.125
  319.7 57.9 %all_to_all.82 = bf16[3,4,800,128]{3,1,0,2:T(4,128)(2,1)S(1)} all-to-all(bf16[3,4,800,128]{3,1,0,2:T(4,128)(2,1)S(1)} %copy.125), channel_id=1, replica_groups=mesh['lvl'=4,'sp'=8] {'lvl'}, dimensions={2} | all-to-all | bytes 4915200 | tf_op jit(solution)/shard_map/all_to_all | solution.py:491
  377.6 68.0 %all_to_all.83 = bf16[8,400,800]{2,1,0:T(8,128)(2,1)} all-to-all(bf16[8,400,800]{2,1,0:T(8,128)(2,1)S(1)} %bitcast.67), channel_id=1, replica_groups=mesh['lvl'=4,'sp'=8] {'sp'}, dimensions={0} | all-to-all | bytes 10240000 | tf_op jit(solution)/shard_map/all_to_all | solution.py:522
  445.6 7.0 all-to-all-start.5
  452.6 4.5 reduce_sum.98
  457.1 4.4 copy.127
  461.5 54.4 %all-to-all-done.5 = bf16[8,400,800]{2,1,0:T(8,128)(2,1)} async-done(((bf16[8,400,800]{2,1,0:T(8,128)(2,1)}), bf16[8,400,800]{2,1,0:T(8,128)(2,1)}, u32[]{:S(2)}, u32[]{:S(2)}) %all-to-all-start.5) | async-done | bytes 5120032 | tf_op jit(solution)/shard_map/all_to_all | solution.py:522
  516.0 6.9 all-to-all-start.3
  522.8 4.5 reduce_sum.100
  527.5 0.7 pad.4.par_ref
  528.2 1.8 copy.126
  530.0 84.2 %all-to-all-done.3 = bf16[3,4,800,128]{3,1,0,2:T(4,128)(2,1)} async-done(((bf16[3,4,800,128]{3,1,0,2:T(4,128)(2,1)}), bf16[3,4,800,128]{3,1,0,2:T(4,128)(2,1)}, u32[]{:S(2)}, u32[]{:S(2)}) %all-to-all-start.3) | async-done | bytes 2457632 | tf_op jit(solution)/shard_map/all_to_all | solution.py:491
  614.2 3.4 copy.128
  617.7 23.5 %shard_map.387 = (f32[3,200,16,128]{3,2,1,0:T(8,128)}, f32[200,128]{1,0:T(8,128)}) custom-call(f32[3,22,200,128]{3,2,1,0:T(8,128)} %get-tuple-element.35.xt_ref, bf16[3,16,200,128]{3,2,1,0:T(8,128)(2,1)} %bitcast.65, bf16[3,16,200,128]{3,2,1,0:T(8,128)(2,1)} %bitcast.61, f32[3,16,200,128]{3,2,1,0:T(8,128)} %get-tuple-element.36.conv_ref, ...), custom_call_target="tpu_custom_call" | custom-call | flops 12288000 | bytes 24576000 | tf_op jit(solution)/shard_map/pallas_call | solution.py:315
  641.1 24.0 %psum.21 = f32[200,6]{1,0:T(8,128)S(1)} all-reduce(f32[200,6]{1,0:T(8,128)} %bitcast.74), channel_id=1, replica_groups=mesh['lvl'=4,'sp'=8] {'sp'}, use_global_device_ids=true, to_apply=%region_3.4 | all-reduce | flops 1200 | bytes 9600 | tf_op jit(solution)/shard_map/psum | solution.py:504
  665.6 4.1 subtract_multiply_fusion.grad_ref
  669.7 2.2 copy-done
  672.1 2.7 collective-permute-start.2
  674.8 2.9 collective-permute-start.3
  678.7 62.0 %psum.23 = f32[4000]{0:T(1024)S(1)} all-reduce(f32[4000]{0:T(1024)S(1)} %pad_maximum_fusion), channel_id=1, replica_groups=mesh['lvl'=4,'sp'=8] {'sp','lvl'}, use_global_device_ids=true, to_apply=%region_9.10 | all-reduce | flops 4000 | bytes 32000 | tf_op jit(solution)/shard_map/psum | solution.py:530
  740.8 0.6 multiply_subtract_fusion.5
  741.4 0.7 multiply_subtract_fusion.3
  742.1 0.6 multiply_subtract_fusion.4
  742.7 0.9 copy-done.14
  743.6 51.5 %shard_map.388 = (f32[3,200,16,128]{3,2,1,0:T(8,128)}, f32[200,128]{1,0:T(8,128)}) custom-call(s32[3,1]{1,0:T(4,128)} %copy.118.crop, f32[3,22,200,128]{3,2,1,0:T(8,128)} %get-tuple-element.35.xt_ref, f32[3,16,200,128]{3,2,1,0:T(8,128)} %copy-done, f32[3,3,200,128]{3,2,1,0:T(8,128)} %copy-done.14, f32[3,3,200,128]{3,2,1,0:T(8,128)} %collective-permute-done.3.dn_ref, ...), custom_call_target="tpu_custom_call" | custom-call | flops 240844800 | bytes 17203200 | tf_op jit(solution)/shard_map/pallas_call | solution.py:403
  795.1 21.6 %psum.22 = f32[200,49]{1,0:T(8,128)S(1)} all-reduce(f32[200,49]{1,0:T(8,128)} %bitcast.73), channel_id=1, replica_groups=mesh['lvl'=4,'sp'=8] {'sp'}, use_global_device_ids=true, to_apply=%region_4.5 | all-reduce | flops 9800 | bytes 78400 | tf_op jit(solution)/shard_map/psum | solution.py:518
  816.7 0.7 copy.139
  817.5 0.7 copy.140
  818.3 0.7 copy.141
  819.0 2.4 convert_reduce_fusion.1
  821.5 3.0 convert_reduce_fusion
  824.6 0.4 copy-done.11
  825.0 2.6 multiply_subtract_fusion.1
  827.7 0.4 copy-done.12
  828.0 0.8 copy-done.13
  828.8 2.6 multiply_subtract_fusion
  (108 shorter events, 2.7 us)
Async XLA Ops:
  7.2 2.6 copy-start.28
  7.2 2.7 copy-start.8
  7.2 210.5 %all-gather.9.cloned.1.call-start = ((), (), s32[]{:S(2)}) async-start(), calls=%async_computation.6 | async-start | bytes 6451200 | tf_op jit(solution)/shard_map/all_gather | solution.py:456
  9.7 208.0 %all-gather.11.cloned.1.call-start = ((), (), s32[]{:S(2)}) async-start(), calls=%async_computation.7 | async-start | bytes 6451200 | tf_op jit(solution)/shard_map/all_gather | solution.py:457
  10.4 6.2 copy-start.4
  10.6 11.4 %collective-permute-start = (bf16[3,3,200,128]{3,2,1,0:T(8,128)(2,1)S(1)}, bf16[3,3,200,128]{3,2,1,0:T(8,128)(2,1)S(1)}, u32[]{:S(2)}, u32[]{:S(2)}) collective-permute-start(bf16[3,3,200,128]{3,2,1,0:T(8,128)(2,1)S(1)} %fusion.3), channel_id=1, source_target_pairs={{0,1},{1,2},{2,3},{3,4},{4,5},{5,6},{6,7},{8,9},{9,10},{10,11},{11... | collective-permute-start | bytes 1382408 | tf_op jit(solution)/shard_map/ppermute | solution.py:438
  12.8 5.5 copy-start.18
  12.8 6.3 copy-start.23
  12.8 6.3 copy-start.21
  12.8 15.3 %collective-permute-start.1 = (bf16[3,3,200,128]{3,2,1,0:T(8,128)(2,1)S(1)}, bf16[3,3,200,128]{3,2,1,0:T(8,128)(2,1)S(1)}, u32[]{:S(2)}, u32[]{:S(2)}) collective-permute-start(bf16[3,3,200,128]{3,2,1,0:T(8,128)(2,1)S(1)} %fusion.2), channel_id=1, source_target_pairs={{1,0},{2,1},{3,2},{4,3},{5,4},{6,5},{7,6},{9,8},{10,9},{11,10},{12... | collective-permute-start | bytes 1382408 | tf_op jit(solution)/shard_map/ppermute | solution.py:439
  22.0 6.1 copy-start.16
  28.1 0.8 copy-start.17
  95.0 59.2 %all-to-all-start = ((bf16[3,16,200,128]{3,2,0,1:T(8,128)(2,1)}), bf16[3,16,200,128]{3,2,0,1:T(8,128)(2,1)S(1)}, u32[]{:S(2)}, u32[]{:S(2)}) async-start(bf16[3,16,200,128]{3,2,0,1:T(8,128)(2,1)} %copy.121), calls=%async_computation | async-start | bytes 4915200 | tf_op jit(solution)/shard_map/all_to_all | solution.py:488
  103.5 57.5 %copy-start.24 = (f32[400]{0:T(512)S(1)}, f32[400]{0:T(512)}, u32[]{:S(2)}) copy-start(f32[400]{0:T(512)} %param.37) | copy-start | bytes 4804
  103.5 57.5 %copy-start.31 = (f32[100]{0:T(128)S(1)}, f32[100]{0:T(128)}, u32[]{:S(2)}) copy-start(f32[100]{0:T(128)} %param.43) | copy-start | bytes 1204
  103.5 57.6 %copy-start.34 = (u32[32]{0:T(128)S(1)}, u32[32]{0:T(128)}, u32[]{:S(2)}) copy-start(u32[32]{0:T(128)} %constant.13) | copy-start | bytes 388
  154.2 60.2 %all-to-all-start.1 = ((bf16[3,16,200,128]{3,2,0,1:T(8,128)(2,1)}), bf16[3,16,200,128]{3,2,0,1:T(8,128)(2,1)}, u32[]{:S(2)}, u32[]{:S(2)}) async-start(bf16[3,16,200,128]{3,2,0,1:T(8,128)(2,1)} %copy.123), calls=%async_computation.1 | async-start | bytes 4915200 | tf_op jit(solution)/shard_map/all_to_all | solution.py:488
  316.6 61.0 %copy-start.2 = (bf16[3200,800]{1,0:T(8,128)(2,1)S(1)}, bf16[3200,800]{1,0:T(8,128)(2,1)}, u32[]{:S(2)}) copy-start(bf16[3200,800]{1,0:T(8,128)(2,1)} %get-tuple-element.45) | copy-start | bytes 15360004
  445.6 70.4 %all-to-all-start.5 = ((bf16[8,400,800]{2,1,0:T(8,128)(2,1)}), bf16[8,400,800]{2,1,0:T(8,128)(2,1)}, u32[]{:S(2)}, u32[]{:S(2)}) async-start(bf16[8,400,800]{2,1,0:T(8,128)(2,1)} %bitcast.66), calls=%async_computation.5 | async-start | bytes 11468800 | tf_op jit(solution)/shard_map/all_to_all | solution.py:522
  452.6 366.4 %all-gather.13.cloned.1.call-start = ((), (), s32[]{:S(2)}) async-start(), calls=%async_computation.8 | async-start | bytes 3584000 | tf_op jit(solution)/shard_map/all_gather | solution.py:526
  516.0 98.3 %all-to-all-start.3 = ((bf16[3,4,800,128]{3,1,0,2:T(4,128)(2,1)}), bf16[3,4,800,128]{3,1,0,2:T(4,128)(2,1)}, u32[]{:S(2)}, u32[]{:S(2)}) async-start(bf16[3,4,800,128]{3,1,0,2:T(4,128)(2,1)} %copy.127), calls=%async_computation.3 | async-start | bytes 4915200 | tf_op jit(solution)/shard_map/all_to_all | solution.py:491
  522.8 298.6 %all-gather.15.cloned.1.call-start = ((), (), s32[]{:S(2)}) async-start(), calls=%async_computation.9 | async-start | bytes 3584000 | tf_op jit(solution)/shard_map/all_gather | solution.py:526
  617.7 47.9 %copy-start.1 = (bf16[3,4,4,200,128]{4,3,1,2,0:T(8,128)(2,1)S(1)}, bf16[3,4,4,200,128]{4,3,1,2,0:T(8,128)(2,1)}, u32[]{:S(2)}) copy-start(bf16[3,4,4,200,128]{4,3,1,2,0:T(8,128)(2,1)} %copy.128) | copy-start | bytes 7372804
  617.7 47.9 %copy-start.15 = (f32[3,16,128]{2,1,0:T(8,128)S(1)}, f32[3,16,128]{2,1,0:T(8,128)}, u32[]{:S(2)}) copy-start(f32[3,16,128]{2,1,0:T(8,128)} %convert_multiply_fusion.mask_ref) | copy-start | bytes 73732
  669.7 2.2 copy-start
  671.9 5.8 copy-start.19
  671.9 6.6 copy-start.20
  671.9 6.8 copy-start.25
  671.9 6.8 copy-start.22
  671.9 68.9 %copy-start.32 = (f32[100]{0:T(128)S(1)}, f32[100]{0:T(128)}, u32[]{:S(2)}) copy-start(f32[100]{0:T(128)} %param.44) | copy-start | bytes 1204
  671.9 68.9 %copy-start.33 = (f32[100]{0:T(128)S(1)}, f32[100]{0:T(128)}, u32[]{:S(2)}) copy-start(f32[100]{0:T(128)} %param.45) | copy-start | bytes 1204
  671.9 69.5 %copy-start.29 = (f32[400]{0:T(512)S(1)}, f32[400]{0:T(512)}, u32[]{:S(2)}) copy-start(f32[400]{0:T(512)} %param.38) | copy-start | bytes 4804
  671.9 69.5 %copy-start.30 = (f32[400]{0:T(512)S(1)}, f32[400]{0:T(512)}, u32[]{:S(2)}) copy-start(f32[400]{0:T(512)} %param.39) | copy-start | bytes 4804
  671.9 70.1 %copy-start.26 = (f32[2,200]{1,0:T(2,128)S(1)}, f32[2,200]{1,0:T(2,128)}, u32[]{:S(2)}) copy-start(f32[2,200]{1,0:T(2,128)} %param.32) | copy-start | bytes 4804
  671.9 70.1 %copy-start.27 = (f32[2,200]{1,0:T(2,128)S(1)}, f32[2,200]{1,0:T(2,128)}, u32[]{:S(2)}) copy-start(f32[2,200]{1,0:T(2,128)} %param.33) | copy-start | bytes 4804
  672.1 70.6 %collective-permute-start.2 = (f32[3,3,200,128]{3,2,1,0:T(8,128)S(1)}, f32[3,3,200,128]{3,2,1,0:T(8,128)S(1)}, u32[]{:S(2)}, u32[]{:S(2)}) collective-permute-start(f32[3,3,200,128]{3,2,1,0:T(8,128)S(1)} %get-tuple-element.153), channel_id=1, source_target_pairs={{0,1},{1,2},{2,3},{3,4},{4,5},{5,6},{6,7},{8,9},{9,10},{10,11},{11... | collective-permute-start | bytes 2764808 | tf_op jit(solution)/shard_map/ppermute | solution.py:438
  674.8 67.9 %collective-permute-start.3 = (f32[3,3,200,128]{3,2,1,0:T(8,128)S(1)}, f32[3,3,200,128]{3,2,1,0:T(8,128)}, u32[]{:S(2)}, u32[]{:S(2)}) collective-permute-start(f32[3,3,200,128]{3,2,1,0:T(8,128)S(1)} %get-tuple-element.152), channel_id=1, source_target_pairs={{1,0},{2,1},{3,2},{4,3},{5,4},{6,5},{7,6},{9,8},{10,9},{11,10},{12... | collective-permute-start | bytes 2764808 | tf_op jit(solution)/shard_map/ppermute | solution.py:439
  742.7 74.8 %copy-start.9 = (f32[200,49]{1,0:T(8,128)S(1)}, f32[200,49]{1,0:T(8,128)}, u32[]{:S(2)}) copy-start(f32[200,49]{1,0:T(8,128)} %copy.119.k_ref) | copy-start | bytes 117604
  742.7 0.9 copy-start.14
  821.4 3.0 copy-start.6
  821.4 3.0 copy-start.3
  821.4 3.1 copy-start.10
  821.5 3.6 copy-start.11
  825.0 2.7 copy-start.7
  825.0 2.7 copy-start.5
  825.0 3.0 copy-start.12
  825.0 3.8 copy-start.13
Sparse Core Ops, SparseCore 0:
  10.5 47.0 all-gather.8
  60.0 43.6 all-gather.10
  457.3 57.4 all-gather.12
  527.5 95.6 all-gather.14

commit v2 on v1

--- a/solution.py
+++ b/solution.py
@@ -283,6 +283,223 @@
     )(pin, back, expand_t, shrink, uplift, offset)
 
 
+def mlp_fused_body(
+    normed, back_ref, et_hbm, w_hbm, up_ref, off_ref,
+    res_out, dn_out, ge_out, gw_out, gu_ref, go_ref,
+    land, stage, et_ref, w_ref, pin, pint, back, backt, res_acc, dn_acc, ge, gw, gstage,
+    in_send, in_recv, out_send, out_recv, load_sem, own_sem, keep_sem, grad_sem,
+):
+    batches, height, channels, width = normed.shape
+    peers = lax.axis_size("lvl")
+    me = lax.axis_index("lvl")
+    rows = height // peers
+    hidden = et_ref.shape[0]
+    last = batches - 1
+
+    loads = [
+        pltpu.make_async_copy(et_hbm, et_ref, load_sem.at[0]),
+        pltpu.make_async_copy(w_hbm, w_ref, load_sem.at[1]),
+    ]
+    for load in loads:
+        load.start()
+
+    barrier = pltpu.get_barrier_semaphore()
+    for k in range(1, peers):
+        pl.semaphore_signal(
+            barrier, inc=1, device_id={"lvl": lax.rem(me + k, peers)},
+            device_id_type=pl.DeviceIdType.MESH,
+        )
+    pl.semaphore_wait(barrier, peers - 1)
+
+    def span_of(at):
+        return pl.ds(pl.multiple_of(at * channels, 8), channels)
+
+    def in_copy(m, k):
+        to = lax.rem(me + k, peers)
+        return pltpu.make_async_remote_copy(
+            src_ref=normed.at[m, pl.ds(to * rows, rows)],
+            dst_ref=land.at[m, :, span_of(me), :],
+            send_sem=in_send.at[m, k], recv_sem=in_recv.at[m, k],
+            device_id={"lvl": to}, device_id_type=pl.DeviceIdType.MESH,
+        )
+
+    def own_in(m):
+        return pltpu.make_async_copy(
+            normed.at[m, pl.ds(me * rows, rows)], land.at[m, :, span_of(me), :], own_sem.at[m]
+        )
+
+    outs = (res_out, dn_out)
+
+    def out_copy(m, k, which):
+        to = lax.rem(me + k, peers)
+        return pltpu.make_async_remote_copy(
+            src_ref=stage.at[which, m, :, span_of(to), :],
+            dst_ref=outs[which].at[m, pl.ds(me * rows, rows)],
+            send_sem=out_send.at[which, m, k], recv_sem=out_recv.at[which, m, k],
+            device_id={"lvl": to}, device_id_type=pl.DeviceIdType.MESH,
+        )
+
+    def own_out(m, which):
+        return pltpu.make_async_copy(
+            stage.at[which, m, :, span_of(me), :],
+            outs[which].at[m, pl.ds(me * rows, rows)],
+            keep_sem.at[which, m],
+        )
+
+    for m in range(batches):
+        own_in(m).start()
+    for k in range(1, peers):
+        in_copy(0, k).start()
+    ge[...] = jnp.zeros_like(ge)
+    gw[...] = jnp.zeros_like(gw)
+    gu_ref[...] = jnp.zeros_like(gu_ref)
+    go_ref[...] = jnp.zeros_like(go_ref)
+    for load in loads:
+        load.wait()
+
+    spans = chunks_of(hidden, 512)
+
+    def grad_copies(index):
+        start, size = spans[index]
+        slot = index % 2
+        return [
+            pltpu.make_async_copy(
+                gstage.at[which, slot, pl.ds(0, size), :],
+                (ge_out, gw_out)[which].at[pl.ds(start, size), :],
+                grad_sem.at[which, slot],
+            )
+            for which in range(2)
+        ]
+
+    def one(m, carry):
+        own_in(m).wait()
+        for k in range(1, peers):
+            in_copy(m, k).wait()
+
+        @pl.when(m == 0)
+        def _():
+            for other in range(1, batches):
+                for k in range(1, peers):
+                    in_copy(other, k).start()
+
+        for r in range(rows):
+            cols = slice(r * width, (r + 1) * width)
+            value = land[m, r]
+            pin[:, cols] = value
+            pint[cols, :] = value.T
+            value = back_ref[m, r]
+            back[:, cols] = value
+            backt[cols, :] = value.T
+        go_ref[...] += jnp.sum(backt[...].astype(jnp.float32), axis=0, keepdims=True)
+        for index, (start, size) in enumerate(spans):
+            span = slice(start, start + size)
+            et = et_ref[span, :]
+            wt = w_ref[span, :]
+            hid = nt(pint[...], et) + up_ref[:, span]
+            dact = nt(backt[...], wt)
+            square = hid * hid
+            t = jnp.tanh(GELU_A * hid * (1.0 + GELU_B * square))
+            half = 0.5 * (1.0 + t)
+            act = (hid * half).astype(jnp.bfloat16)
+            slope = half + 0.5 * hid * (1.0 - t * t) * (
+                GELU_A * (1.0 + 3.0 * GELU_B * square)
+            )
+            dhid = (slope * dact).astype(jnp.bfloat16)
+            res_part = nn(act, wt)
+            dn_part = nn(dhid, et)
+            if index == 0:
+                res_acc[...] = res_part
+                dn_acc[...] = dn_part
+            else:
+                res_acc[...] += res_part
+                dn_acc[...] += dn_part
+            ge[:, span] += nn(pin[...], dhid)
+            gw[:, span] += nn(back[...], act)
+            gu_ref[:, span] += jnp.sum(dhid.astype(jnp.float32), axis=0, keepdims=True)
+
+            @pl.when(m == last)
+            def _():
+                if index >= 2:
+                    for copy in grad_copies(index - 2):
+                        copy.wait()
+                gstage[0, index % 2, :size, :] = ge[:, span].astype(jnp.bfloat16).T
+                gstage[1, index % 2, :size, :] = gw[:, span].astype(jnp.bfloat16).T
+                for copy in grad_copies(index):
+                    copy.start()
+
+        for r in range(rows):
+            cols = slice(r * width, (r + 1) * width)
+            stage[0, m, r] = (res_acc[cols, :] + off_ref[...]).astype(jnp.bfloat16).T
+            stage[1, m, r] = dn_acc[cols, :].astype(jnp.bfloat16).T
+        for which in range(2):
+            for k in range(1, peers):
+                out_copy(m, k, which).start()
+            own_out(m, which).start()
+        return carry
+
+    lax.fori_loop(0, batches, one, 0)
+    for index in range(max(len(spans) - 2, 0), len(spans)):
+        for copy in grad_copies(index):
+            copy.wait()
+    for m in range(batches):
+        for which in range(2):
+            own_out(m, which).wait()
+            for k in range(1, peers):
+                out_copy(m, k, which).wait()
+
+
+def mlp_fused(normed, back, expand_t, shrink, uplift, offset, ident):
+    batches, height, channels, width = normed.shape
+    peers = lax.axis_size("lvl")
+    rows = height // peers
+    hidden, every = expand_t.shape
+    pixels = rows * width
+    bf, f32 = jnp.bfloat16, jnp.float32
+    hbm = pl.BlockSpec(memory_space=pl.ANY)
+    vmem = pl.BlockSpec(memory_space=pltpu.VMEM)
+    dma = pltpu.SemaphoreType.DMA
+    chunk = min(512, hidden)
+    return pl.pallas_call(
+        mlp_fused_body,
+        in_specs=[hbm, vmem, hbm, hbm, vmem, vmem],
+        out_specs=[hbm, hbm, hbm, hbm, vmem, vmem],
+        out_shape=[
+            jax.ShapeDtypeStruct(normed.shape, bf),
+            jax.ShapeDtypeStruct(normed.shape, bf),
+            jax.ShapeDtypeStruct((hidden, every), bf),
+            jax.ShapeDtypeStruct((hidden, every), bf),
+            jax.ShapeDtypeStruct((1, hidden), f32),
+            jax.ShapeDtypeStruct((1, every), f32),
+        ],
+        scratch_shapes=[
+            pltpu.VMEM((batches, rows, every, width), bf),
+            pltpu.VMEM((2, batches, rows, every, width), bf),
+            pltpu.VMEM((hidden, every), bf),
+            pltpu.VMEM((hidden, every), bf),
+            pltpu.VMEM((every, pixels), bf),
+            pltpu.VMEM((pixels, every), bf),
+            pltpu.VMEM((every, pixels), bf),
+            pltpu.VMEM((pixels, every), bf),
+            pltpu.VMEM((pixels, every), f32),
+            pltpu.VMEM((pixels, every), f32),
+            pltpu.VMEM((every, hidden), f32),
+            pltpu.VMEM((every, hidden), f32),
+            pltpu.VMEM((2, 2, chunk, every), bf),
+            dma((batches, peers)), dma((batches, peers)),
+            dma((2, batches, peers)), dma((2, batches, peers)),
+            dma((2,)), dma((batches,)), dma((2, batches)), dma((2, 2)),
+        ],
+        compiler_params=pltpu.CompilerParams(
+            vmem_limit_bytes=63 * 1024 * 1024, collective_id=ident, has_side_effects=True
+        ),
+        cost_estimate=pl.CostEstimate(
+            flops=12 * batches * pixels * every * hidden,
+            bytes_accessed=8 * every * hidden,
+            transcendentals=batches * pixels * hidden,
+        ),
+    )(normed, back, expand_t, shrink, uplift, offset)
+
+
 def sums_body(xt_ref, res_ref, dn_ref, conv_ref, mask_ref, par_ref, out_ref, stat_ref, scr):
     batches, height = res_ref.shape[:2]
     width = res_ref.shape[3]
@@ -491,13 +708,17 @@
         return lax.all_to_all(v, "lvl", split_axis=2, concat_axis=1, tiled=True)
 
     pixel_back = to_pixels(dres)
-    pixel_in = to_pixels(normed)
-    result, grad_normed, grad_expand, grad_shrink, grad_uplift, grad_offset = mlp(
-        pixel_in, pixel_back, expand_all, shrink_all,
-        uplift_all.astype(f32)[None], offset_all.astype(f32)[None],
-    )
-    result = to_channels(result)
-    grad_normed = to_channels(grad_normed)
+    biases = (uplift_all.astype(f32)[None], offset_all.astype(f32)[None])
+    if channels % 8 == 0:
+        result, grad_normed, grad_expand, grad_shrink, grad_uplift, grad_offset = mlp_fused(
+            normed, pixel_back, expand_all, shrink_all, *biases, 1
+        )
+    else:
+        result, grad_normed, grad_expand, grad_shrink, grad_uplift, grad_offset = mlp(
+            to_pixels(normed), pixel_back, expand_all, shrink_all, *biases
+        )
+        result = to_channels(result)
+        grad_normed = to_channels(grad_normed)
     params = jnp.concatenate([mean, rho], axis=1)
     params = jnp.pad(params, ((0, 0), (0, 128 - params.shape[1])))
     block_output, local = output_and_sums(xt, result, grad_normed, conv, mask_cells, params)

time: 851 us -> 684 us (0.80)
  waiting for transfers between devices: 225 us -> 70.2 us
  Pallas kernels: 220 us -> 288 us
  blocking collectives: 267 us -> 215 us
  local copies, waits for them, and re-layouts: 37 us -> 20.1 us
  starting transfers between devices: 37.2 us -> 23.1 us
    all_to_all x1 -> x0, waiting for transfers between devices: 84.2 us -> none  [to_channels(): return lax.all_to_all(v, 'lvl', split_axis=2, concat_axis=1, tiled=True)]
    all_to_all x2 -> x1, waiting for transfers between devices: 78 us -> 0.01 us  [to_pixels(): return lax.all_to_all(v, 'lvl', split_axis=1, concat_axis=2, tiled=True)]
    pallas_call x1, Pallas kernels: 98.9 us -> 167 us  [mlp_fused(): pl.pallas_call(mlp_fused_body, in_specs=[hbm, vmem, hbm, hbm, vmem, vmem]...]
    all_to_all x1 -> x0, blocking collectives: 57.9 us -> none  [to_channels(): return lax.all_to_all(v, 'lvl', split_axis=2, concat_axis=1, tiled=True)]
    all_to_all x1, blocking collectives: 68 us -> 78.6 us  [own_share(): lax.all_to_all(partial.reshape(sp, rows, partial.shape[1]), 'sp', split_a...]
  transfers between devices with their start and end apart: 12 -> 10, of which waited for: 6 -> 3; matrix products, arithmetic and copies ran while one was open for 6% -> 6% of each run, Pallas kernels for 14% -> 18%
where the time goes in v2:
time: 684 us; the launch traced here: 670 us
  Pallas kernels  288 us (42%)
  blocking collectives  215 us (31%)
  waiting for transfers between devices  70.2 us (10%)
  other arithmetic  35.9 us (5%)
  starting transfers between devices  23.1 us (3%)
  local copies, waits for them, and re-layouts  20.1 us (3%)
  between operations  17.6 us (3%)
    pallas_call x1, Pallas kernels, mlp_fused(): pl.pallas_call(mlp_fused_body, in_specs=[hbm, vmem, hbm, hbm, vmem, vmem]...  167 us
    all_to_all x1, blocking collectives, own_share(): lax.all_to_all(partial.reshape(sp, rows, partial.shape[1]), 'sp', split_a...  78.6 us
    all_to_all x1, waiting for transfers between devices, own_share(): lax.all_to_all(partial.reshape(sp, rows, partial.shape[1]), 'sp', split_a...  58.8 us
    psum x1, blocking collectives, on_device(): lax.psum(jnp.concatenate([grad_uplift[0], grad_offset[0]]), ('sp', 'lvl'))  53.9 us
    pallas_call x1, Pallas kernels, conv_backward(): pl.pallas_call(conv_back_body, grid_spec=pltpu.PrefetchScalarGridSpec(num...  51.5 us
    pallas_call x1, Pallas kernels, conv_forward(): pl.pallas_call(conv_body, grid_spec=pltpu.PrefetchScalarGridSpec(num_scal...  46.6 us
    psum x1, blocking collectives, on_device(): both = lax.psum(local[:, :2 * batches], 'sp')  24.8 us
    unnamed x1, blocking collectives  24.8 us
  transfers between devices with their start and end apart: 10, of which 3 were waited for; matrix products, arithmetic and copies ran while one was open for 6% of the time, Pallas kernels for 18%

profile of v2, /device:TPU:30, one launch (start us, length us, event | category | flops | bytes accessed | tf_op | source)
XLA Modules:
  0.0 670.1 jit_solution(7837139843379504536)
XLA Ops:
  7.2 2.4 convert_bitcast_fusion
  9.7 0.9 convert_element_type.74
  10.9 2.1 fusion.17
  13.0 0.2 fusion.3
  13.2 1.9 collective-permute-start
  15.1 0.2 fusion.2
  15.3 3.6 collective-permute-start.1
  18.9 0.7 copy.103.crop
  19.6 0.7 copy.104.k_ref
  20.4 0.7 convert_multiply_fusion.mask_ref
  21.1 8.0 %collective-permute-done.up_ref = bf16[3,3,200,128]{3,2,1,0:T(8,128)(2,1)S(1)} collective-permute-done((bf16[3,3,200,128]{3,2,1,0:T(8,128)(2,1)S(1)}, bf16[3,3,200,128]{3,2,1,0:T(8,128)(2,1)S(1)}, u32[]{:S(2)}, u32[]{:S(2)}) %collective-permute-start) | collective-permute-done | bytes 460832 | tf_op jit(solution)/shard_map/ppermute | solution.py:655
  29.1 3.4 collective-permute-done.1.dn_ref
  32.5 0.8 copy-done.15
  33.2 46.6 %shard_map.385 = (f32[3,16,200,128]{3,2,1,0:T(8,128)}, f32[3,22,200,128]{3,2,1,0:T(8,128)}, bf16[3,16,200,128]{3,2,1,0:T(8,128)(2,1)}, f32[200,128]{1,0:T(8,128)}) custom-call(s32[3,1]{1,0:T(4,128)} %copy.103.crop, bf16[3,200,16,128]{3,2,1,0:T(8,128)(2,1)} %x_ref.1, bf16[3,200,16,128]{3,2,1,0:T(8,128)(2,1)} %cot_ref.3, bf16[3,3,200,128]{3,2,1,0:T(8,128)(2,1)} %copy-done.14, ...), custom_call_target="tpu_custom_call" | custom-call | flops 120422400 | bytes 36864000 | tf_op jit(solution)/shard_map/pallas_call | solution.py:119
  79.8 3.3 copy.106
  83.1 5.2 all-to-all-start
  88.4 0.6 dynamic-slice
  90.3 0.3 dynamic-update-slice
  90.5 0.2 dynamic-update-slice.1
  90.7 24.8 %all-reduce.3 = (bf16[3200]{0:T(1024)(128)(2,1)S(1)}, bf16[800]{0:T(1024)(128)(2,1)S(1)}) all-reduce(bf16[3200]{0:T(1024)(128)(2,1)S(1)} %dynamic-update-slice, bf16[800]{0:T(1024)(128)(2,1)S(1)} %dynamic-update-slice.1), channel_id=1, replica_groups=mesh['lvl'=4,'sp'=8] {'sp'}, use_global_device_ids=true, to_apply=%add.1 | all-reduce | flops 4000 | bytes 16000
  115.5 0.6 reshape.130.up_ref
  116.1 0.6 reshape.131.off_ref
  116.8 11.2 %all-gather.3 = f32[8,200,12]{1,2,0:T(8,128)S(1)} all-gather(f32[1,200,12]{1,2,0:T(8,128)S(1)} %copy.105), channel_id=2, replica_groups=mesh['lvl'=4,'sp'=8] {'sp'}, dimensions={0}, use_global_device_ids=true | all-gather | bytes 86400 | tf_op jit(solution)/shard_map/all_gather | solution.py:687
  128.1 5.3 add_convert_fusion.normed
  133.3 1.7 copy.107
  135.0 166.8 %shard_map.386 = (bf16[3,16,200,128]{3,2,1,0:T(8,128)(2,1)}, bf16[3,16,200,128]{3,2,1,0:T(8,128)(2,1)}, bf16[3200,800]{1,0:T(8,128)(2,1)}, bf16[3200,800]{1,0:T(...) custom-call(bf16[3,16,200,128]{3,2,1,0:T(8,128)(2,1)} %add_convert_fusion.normed, bf16[3,4,800,128]{3,2,1,0:T(8,128)(2,1)} %bitcast.55, ...), custom_call_target="tpu_custom_call" | custom-call | flops 47185920000 | bytes 20480000 | tf_op jit(solution)/shard_map/pallas_call | solution.py:462
  301.8 78.6 %all_to_all.28 = bf16[8,400,800]{2,1,0:T(8,128)(2,1)} all-to-all(bf16[8,400,800]{2,1,0:T(8,128)(2,1)} %bitcast.51), channel_id=1, replica_groups=mesh['lvl'=4,'sp'=8] {'sp'}, dimensions={0} | all-to-all | bytes 10240000 | tf_op jit(solution)/shard_map/all_to_all | solution.py:743
  380.4 6.7 all-to-all-start.2
  387.1 4.5 reduce_sum.98
  391.6 58.8 %all-to-all-done.2 = bf16[8,400,800]{2,1,0:T(8,128)(2,1)} async-done(((bf16[8,400,800]{2,1,0:T(8,128)(2,1)}), bf16[8,400,800]{2,1,0:T(8,128)(2,1)}, u32[]{:S(2)}, u32[]{:S(2)}) %all-to-all-start.2) | async-done | bytes 5120032 | tf_op jit(solution)/shard_map/all_to_all | solution.py:743
  450.4 4.5 reduce_sum.100
  455.0 0.1 copy.108
  455.1 0.7 pad.4.par_ref
  455.8 23.6 %shard_map.387 = (f32[3,200,16,128]{3,2,1,0:T(8,128)}, f32[200,128]{1,0:T(8,128)}) custom-call(f32[3,22,200,128]{3,2,1,0:T(8,128)} %get-tuple-element.35.xt_ref, bf16[3,16,200,128]{3,2,1,0:T(8,128)(2,1)} %get-tuple-element.39.res_ref, bf16[3,16,200,128]{3,2,1,0:T(8,128)(2,1)} %get-tuple-element.40.dn_ref, f32[3,16,200,128]{3,2,1,0:T(8,128)} %get-tuple-element.36.conv_ref, ...), custom_call_target="tpu_custom_call" | custom-call | flops 12288000 | bytes 24576000 | tf_op jit(solution)/shard_map/pallas_call | solution.py:532
  479.4 24.8 %psum.21 = f32[200,6]{1,0:T(8,128)S(1)} all-reduce(f32[200,6]{1,0:T(8,128)} %bitcast.57), channel_id=1, replica_groups=mesh['lvl'=4,'sp'=8] {'sp'}, use_global_device_ids=true, to_apply=%region_3.4 | all-reduce | flops 1200 | bytes 9600 | tf_op jit(solution)/shard_map/psum | solution.py:725
  504.2 0.2 slice_reduce_fusion
  504.4 0.1 copy.110
  504.5 0.1 copy.109
  504.6 4.1 subtract_multiply_fusion.grad_ref
  508.7 2.2 copy-done
  511.0 0.1 fusion.16
  511.1 2.7 collective-permute-start.2
  513.8 2.9 collective-permute-start.3
  516.7 0.1 copy.115
  517.6 0.1 copy.113
  517.8 53.9 %psum.23 = f32[4000]{0:T(1024)S(1)} all-reduce(f32[4000]{0:T(1024)S(1)} %pad_maximum_fusion), channel_id=1, replica_groups=mesh['lvl'=4,'sp'=8] {'sp','lvl'}, use_global_device_ids=true, to_apply=%region_9.10 | all-reduce | flops 4000 | bytes 32000 | tf_op jit(solution)/shard_map/psum | solution.py:751
  571.8 0.6 multiply_subtract_fusion.5
  572.4 0.7 multiply_subtract_fusion.3
  573.1 0.6 multiply_subtract_fusion.4
  573.7 0.9 copy-done.12
  574.6 51.5 %shard_map.388 = (f32[3,200,16,128]{3,2,1,0:T(8,128)}, f32[200,128]{1,0:T(8,128)}) custom-call(s32[3,1]{1,0:T(4,128)} %copy.103.crop, f32[3,22,200,128]{3,2,1,0:T(8,128)} %get-tuple-element.35.xt_ref, f32[3,16,200,128]{3,2,1,0:T(8,128)} %copy-done, f32[3,3,200,128]{3,2,1,0:T(8,128)} %copy-done.12, f32[3,3,200,128]{3,2,1,0:T(8,128)} %collective-permute-done.3.dn_ref, ...), custom_call_target="tpu_custom_call" | custom-call | flops 240844800 | bytes 17203200 | tf_op jit(solution)/shard_map/pallas_call | solution.py:620
  626.1 21.4 %psum.22 = f32[200,49]{1,0:T(8,128)S(1)} all-reduce(f32[200,49]{1,0:T(8,128)} %bitcast.56), channel_id=1, replica_groups=mesh['lvl'=4,'sp'=8] {'sp'}, use_global_device_ids=true, to_apply=%region_4.5 | all-reduce | flops 9800 | bytes 78400 | tf_op jit(solution)/shard_map/psum | solution.py:739
  647.5 0.7 copy.118
  648.2 0.1 multiply_subtract_fusion.2
  648.3 0.7 copy.119
  649.1 0.7 copy.120
  649.8 2.4 convert_reduce_fusion.1
  652.3 3.0 convert_reduce_fusion
  655.2 0.1 copy-done.8
  655.4 0.4 copy-done.9
  655.8 2.6 multiply_subtract_fusion.1
  658.5 0.4 copy-done.10
  658.8 0.8 copy-done.11
  659.6 2.6 multiply_subtract_fusion
  (95 shorter events, 0.9 us)
Async XLA Ops:
  7.2 2.5 copy-start.3
  7.2 127.8 %all-gather.9.cloned.1.call-start = ((), (), s32[]{:S(2)}) async-start(), calls=%async_computation.3 | async-start | bytes 6451200 | tf_op jit(solution)/shard_map/all_gather | solution.py:673
  9.7 1.0 copy-start.27
  9.7 125.3 %all-gather.11.cloned.1.call-start = ((), (), s32[]{:S(2)}) async-start(), calls=%async_computation.4 | async-start | bytes 6451200 | tf_op jit(solution)/shard_map/all_gather | solution.py:674
  13.0 6.6 copy-start.17
  13.0 7.4 %copy-start.20 = (s32[3,16,128]{2,1,0:T(8,128)S(1)}, s32[3,16,128]{2,1,0:T(8,128)}, u32[]{:S(2)}) copy-start(s32[3,16,128]{2,1,0:T(8,128)} %param.25) | copy-start | bytes 73732
  13.2 15.9 %collective-permute-start = (bf16[3,3,200,128]{3,2,1,0:T(8,128)(2,1)S(1)}, bf16[3,3,200,128]{3,2,1,0:T(8,128)(2,1)S(1)}, u32[]{:S(2)}, u32[]{:S(2)}) collective-permute-start(bf16[3,3,200,128]{3,2,1,0:T(8,128)(2,1)S(1)} %fusion.3), channel_id=1, source_target_pairs={{0,1},{1,2},{2,3},{3,4},{4,5},{5,6},{6,7},{8,9},{9,10},{10,11},{11... | collective-permute-start | bytes 1382408 | tf_op jit(solution)/shard_map/ppermute | solution.py:655
  15.3 17.2 %collective-permute-start.1 = (bf16[3,3,200,128]{3,2,1,0:T(8,128)(2,1)S(1)}, bf16[3,3,200,128]{3,2,1,0:T(8,128)(2,1)S(1)}, u32[]{:S(2)}, u32[]{:S(2)}) collective-permute-start(bf16[3,3,200,128]{3,2,1,0:T(8,128)(2,1)S(1)} %fusion.2), channel_id=1, source_target_pairs={{1,0},{2,1},{3,2},{4,3},{5,4},{6,5},{7,6},{9,8},{10,9},{11,10},{12... | collective-permute-start | bytes 1382408 | tf_op jit(solution)/shard_map/ppermute | solution.py:656
  29.1 3.4 copy-start.14
  32.5 0.8 copy-start.15
  83.1 5.3 copy-start.23
  83.1 5.3 copy-start.30
  83.1 5.3 copy-start.33
  83.1 33.6 %copy-start.22 = (f32[2,200]{1,0:T(2,128)S(1)}, f32[2,200]{1,0:T(2,128)}, u32[]{:S(2)}) copy-start(f32[2,200]{1,0:T(2,128)} %param.31) | copy-start | bytes 4804
  83.1 33.6 %copy-start.16 = (f32[200,128]{1,0:T(8,128)S(1)}, f32[200,128]{1,0:T(8,128)}, u32[]{:S(2)}) copy-start(f32[200,128]{1,0:T(8,128)} %get-tuple-element.37) | copy-start | bytes 307204
  83.1 50.2 %all-to-all-start = ((bf16[3,16,200,128]{3,2,0,1:T(8,128)(2,1)}), bf16[3,16,200,128]{3,2,0,1:T(8,128)(2,1)S(1)}, u32[]{:S(2)}, u32[]{:S(2)}) async-start(bf16[3,16,200,128]{3,2,0,1:T(8,128)(2,1)} %copy.106), calls=%async_computation | async-start | bytes 4915200 | tf_op jit(solution)/shard_map/all_to_all | solution.py:705
  380.4 70.0 %all-to-all-start.2 = ((bf16[8,400,800]{2,1,0:T(8,128)(2,1)}), bf16[8,400,800]{2,1,0:T(8,128)(2,1)}, u32[]{:S(2)}, u32[]{:S(2)}) async-start(bf16[8,400,800]{2,1,0:T(8,128)(2,1)} %bitcast.50), calls=%async_computation.2 | async-start | bytes 11468800 | tf_op jit(solution)/shard_map/all_to_all | solution.py:743
  387.1 262.7 %all-gather.13.cloned.1.call-start = ((), (), s32[]{:S(2)}) async-start(), calls=%async_computation.5 | async-start | bytes 3584000 | tf_op jit(solution)/shard_map/all_gather | solution.py:747
  391.6 260.6 %all-gather.15.cloned.1.call-start = ((), (), s32[]{:S(2)}) async-start(), calls=%async_computation.6 | async-start | bytes 3584000 | tf_op jit(solution)/shard_map/all_gather | solution.py:747
  455.8 48.8 %copy-start.1 = (bf16[3,16,200,128]{3,2,1,0:T(8,128)(2,1)S(1)}, bf16[3,16,200,128]{3,2,1,0:T(8,128)(2,1)}, u32[]{:S(2)}) copy-start(bf16[3,16,200,128]{3,2,1,0:T(8,128)(2,1)} %get-tuple-element.40.dn_ref) | copy-start | bytes 7372804
  455.8 48.8 %copy-start.13 = (f32[3,16,128]{2,1,0:T(8,128)S(1)}, f32[3,16,128]{2,1,0:T(8,128)}, u32[]{:S(2)}) copy-start(f32[3,16,128]{2,1,0:T(8,128)} %convert_multiply_fusion.mask_ref) | copy-start | bytes 73732
  508.7 2.2 copy-start
  510.9 5.8 copy-start.18
  510.9 6.6 copy-start.19
  510.9 6.8 %copy-start.24 = (f32[1,800]{1,0:T(1,128)S(1)}, f32[1,800]{1,0:T(1,128)}, u32[]{:S(2)}) copy-start(f32[1,800]{1,0:T(1,128)} %get-tuple-element.47) | copy-start | bytes 9604
  510.9 6.8 %copy-start.21 = (f32[1,3200]{1,0:T(1,128)S(1)}, f32[1,3200]{1,0:T(1,128)}, u32[]{:S(2)}) copy-start(f32[1,3200]{1,0:T(1,128)} %get-tuple-element.46) | copy-start | bytes 38404
  510.9 60.8 %copy-start.31 = (f32[100]{0:T(128)S(1)}, f32[100]{0:T(128)}, u32[]{:S(2)}) copy-start(f32[100]{0:T(128)} %param.44) | copy-start | bytes 1204
  510.9 60.8 %copy-start.32 = (f32[100]{0:T(128)S(1)}, f32[100]{0:T(128)}, u32[]{:S(2)}) copy-start(f32[100]{0:T(128)} %param.45) | copy-start | bytes 1204
  511.0 61.4 %copy-start.28 = (f32[400]{0:T(512)S(1)}, f32[400]{0:T(512)}, u32[]{:S(2)}) copy-start(f32[400]{0:T(512)} %param.38) | copy-start | bytes 4804
  511.0 61.4 %copy-start.29 = (f32[400]{0:T(512)S(1)}, f32[400]{0:T(512)}, u32[]{:S(2)}) copy-start(f32[400]{0:T(512)} %param.39) | copy-start | bytes 4804
  511.0 62.1 %copy-start.25 = (f32[2,200]{1,0:T(2,128)S(1)}, f32[2,200]{1,0:T(2,128)}, u32[]{:S(2)}) copy-start(f32[2,200]{1,0:T(2,128)} %param.32) | copy-start | bytes 4804
  511.0 62.1 %copy-start.26 = (f32[2,200]{1,0:T(2,128)S(1)}, f32[2,200]{1,0:T(2,128)}, u32[]{:S(2)}) copy-start(f32[2,200]{1,0:T(2,128)} %param.33) | copy-start | bytes 4804
  511.1 62.6 %collective-permute-start.2 = (f32[3,3,200,128]{3,2,1,0:T(8,128)S(1)}, f32[3,3,200,128]{3,2,1,0:T(8,128)S(1)}, u32[]{:S(2)}, u32[]{:S(2)}) collective-permute-start(f32[3,3,200,128]{3,2,1,0:T(8,128)S(1)} %get-tuple-element.153), channel_id=1, source_target_pairs={{0,1},{1,2},{2,3},{3,4},{4,5},{5,6},{6,7},{8,9},{9,10},{10,11},{11... | collective-permute-start | bytes 2764808 | tf_op jit(solution)/shard_map/ppermute | solution.py:655
  513.8 59.9 %collective-permute-start.3 = (f32[3,3,200,128]{3,2,1,0:T(8,128)S(1)}, f32[3,3,200,128]{3,2,1,0:T(8,128)}, u32[]{:S(2)}, u32[]{:S(2)}) collective-permute-start(f32[3,3,200,128]{3,2,1,0:T(8,128)S(1)} %get-tuple-element.152), channel_id=1, source_target_pairs={{1,0},{2,1},{3,2},{4,3},{5,4},{6,5},{7,6},{9,8},{10,9},{11,10},{12... | collective-permute-start | bytes 2764808 | tf_op jit(solution)/shard_map/ppermute | solution.py:656
  573.7 74.5 %copy-start.7 = (f32[200,49]{1,0:T(8,128)S(1)}, f32[200,49]{1,0:T(8,128)}, u32[]{:S(2)}) copy-start(f32[200,49]{1,0:T(8,128)} %copy.104.k_ref) | copy-start | bytes 117604
  573.7 0.9 copy-start.12
  652.2 3.0 copy-start.5
  652.2 3.0 copy-start.2
  652.2 3.1 copy-start.8
  652.2 3.6 copy-start.9
  655.8 2.7 copy-start.6
  655.8 2.7 copy-start.4
  655.8 3.0 copy-start.10
  655.8 3.8 copy-start.11
Sparse Core Ops, SparseCore 0:
  10.5 48.7 all-gather.8
  61.8 43.4 all-gather.10
  391.7 57.4 all-gather.12
  455.1 57.4 all-gather.14
